TPU v7x, 128 devices: a whole 4x4x4 slice. The times are simulated.
128 devices in a mesh: chan: 16 (over y, z_hi, core), seq: 8 (over x, z_lo).
Axes of the slice: x: 4, y: 4, z: 4 (z_hi: 2, z_lo: 2; z = z_hi * 2 + z_lo), core: 2. Of those that a mesh axis runs over, the one named last changes fastest.
Arguments:
- value: bfloat16 [16, 128, 32768], P('seq', 'chan'), may hold values from -6 to 6
- gate_in: bfloat16 [16, 128, 32768], P('seq', 'chan'), may hold values from -6 to 6
- gate_out: bfloat16 [16, 128, 32768], P('seq', 'chan'), may hold values from -6 to 6
- cotangent: bfloat16 [16, 128, 32768], P('seq', 'chan'), may hold values from -6 to 6
- skip_gain: float32 [128], P('chan'), may hold values from 0.25 to 1.5
- weight_in: float32 [64, 33], replicated, may hold values from -1 to 1
- bias_in: float32 [64], replicated, may hold values from -1 to 1
- weight_mid: float32 [2, 64, 64], replicated, may hold values from -0.75 to 0.75
- bias_mid: float32 [2, 64], replicated, may hold values from -1 to 1
- weight_out: float32 [128, 64], replicated, may hold values from -0.75 to 0.75
- decay_rate: float32 [128], replicated, may hold values from 3 to 15
Outputs:
- grad_value: bfloat16 [16, 128, 32768], P('seq', 'chan')
- grad_gate_in: bfloat16 [16, 128, 32768], P('seq', 'chan')
- grad_gate_out: bfloat16 [16, 128, 32768], P('seq', 'chan')
- grad_skip: float32 [128], P('chan')
- grad_weight_in: float32 [64, 33], replicated
- grad_bias_in: float32 [64], replicated
- grad_weight_mid: float32 [2, 64, 64], replicated
- grad_bias_mid: float32 [2, 64], replicated
- grad_weight_out: float32 [128, 64], replicated
- grad_rate: float32 [128], replicated
All inputs are finite; a program needn't handle non-finite values.
Results may differ from a plain program's by a relative error of at most 0.009.
Values sent between devices are 32-bit elements; how exact they have to be, the bound alone decides.
A program may use at most 128 MiB of HBM per device.

v0:
```python
import functools
import math

import jax
import jax.numpy as jnp
import numpy as np
from jax import lax
from jax.experimental import pallas as pl
from jax.experimental.pallas import tpu as pltpu
from jax.sharding import PartitionSpec as P

EPSILON = 1e-06
HIGHEST = lax.Precision.HIGHEST
L = 32768
A = 256
B = 128
CH = 8
NSEQ = 8
NCHAN = 16
ABLK = A // NSEQ
TB = L // NSEQ
CHUNK = 1024
LOW = jnp.bfloat16
F32 = jnp.float32
MESH = pl.DeviceIdType.MESH


def band_table(length, bands):
    highest = length / 4.0
    return np.array(
        [math.floor(highest ** (number / (bands - 1)) + 0.5) for number in range(bands)], np.int64
    )


def row_constants():
    freq = np.zeros((48, 128), np.int32)
    off = np.zeros((48, 128), np.int32)
    bands = band_table(L, 16)
    freq[1:17] = bands[:, None]
    off[1:17] = L // 4
    freq[17:33] = bands[:, None]
    return np.stack([freq, off])


def transform_tables():
    k = np.arange(A)[:, None]
    rows = 2.0 * np.pi * (((4 * k + 1) * np.arange(A)[None, :]) % 1024) / 1024.0
    w1 = np.concatenate([np.cos(rows), -np.sin(rows)], axis=0)
    turn = 2.0 * np.pi * (((4 * k + 1) * np.arange(B)[None, :]) % (4 * L)) / (4.0 * L)
    q = np.arange(B)
    cols = 2.0 * np.pi * ((q[:, None] * q[None, :]) % B) / B
    c, s = np.cos(cols), np.sin(cols)
    fwd = np.block([[c, -s], [s, c]])
    inv = np.block([[c, s], [-s, c]])
    low = np.dtype(LOW)
    return (
        w1.astype(low),
        w1.T.astype(low),
        fwd.astype(low),
        inv.astype(low),
        np.stack([np.cos(turn), np.sin(turn)]).astype(np.float32),
    )


def poly_fit():
    x = (np.cos(np.pi * (np.arange(64) + 0.5) / 64) + 1) / 2 * (np.pi / 2 * 1.002) ** 2
    r = np.sqrt(x)
    sin_c = np.polynomial.polynomial.polyfit(x, np.sin(r) / r, 5)
    cos_c = np.polynomial.polynomial.polyfit(x, np.cos(r), 6)
    return [float(v) for v in sin_c], [float(v) for v in cos_c]


SIN_C, COS_C = poly_fit()


def horner(x, coefs):
    acc = jnp.full_like(x, coefs[-1])
    for value in coefs[-2::-1]:
        acc = acc * x + value
    return acc


def sin_small(r):
    return r * horner(r * r, SIN_C)


def sin_cos(z):
    n = jnp.floor(z * (1.0 / math.pi) + 0.5)
    r = z - n * 3.140625
    r = r - n * 9.67653589793e-4
    half = n * 0.5
    sign = 1.0 - 4.0 * (half - jnp.floor(half))
    r2 = r * r
    return sign * (r * horner(r2, SIN_C)), sign * horner(r2, COS_C)


def dot_full(x, y):
    return jnp.dot(x, y, precision=HIGHEST, preferred_element_type=F32)


def dot_nt(x, y, precision=None):
    return lax.dot_general(x, y, (((1,), (1,)), ((), ())), precision=precision, preferred_element_type=F32)


def dot_tn(x, y, precision=None):
    return lax.dot_general(x, y, (((0,), (0,)), ((), ())), precision=precision, preferred_element_type=F32)


def low_dot(x, y):
    return jnp.dot(x, y, preferred_element_type=F32)


def split(x):
    hi = x.astype(LOW)
    return hi, (x - hi.astype(F32)).astype(LOW)


def iota(shape, dim):
    return lax.broadcasted_iota(jnp.int32, shape, dim)


def to_column(row, size, shift):
    n = row.shape[1]
    pick = iota((size, n), 0) + shift == iota((size, n), 1)
    return jnp.sum(jnp.where(pick, jnp.broadcast_to(row, (size, n)), 0.0), axis=1, keepdims=True)


def to_row(col):
    n = col.shape[0]
    pick = iota((n, n), 0) == iota((n, n), 1)
    return jnp.sum(jnp.where(pick, jnp.broadcast_to(col, (n, n)), 0.0), axis=0, keepdims=True)


def repeat_matrix(rows, period, times):
    shape = (rows, period * times)
    j = iota(shape, 1)
    hit = j == iota(shape, 0)
    for m in range(1, times):
        hit = hit | (j == iota(shape, 0) + m * period)
    return jnp.where(hit, 1.0, 0.0)


def hi_hi_lo(w, period):
    hi = w.astype(LOW).astype(F32)
    lane = iota(w.shape, 1)
    out = jnp.where(lane < 2 * period, hi, jnp.where(lane < 3 * period, w - hi, 0.0))
    return out.astype(LOW)


class Refs:
    def __init__(self, **refs):
        self.__dict__.update(refs)


def prepare_weights(r, chan):
    first = jnp.where(iota((8, 64), 0) == 1, jnp.broadcast_to(r.b_in[...], (8, 64)), 0.0)
    r.w_pad[0:32, :] = r.w_in[0:32, :]
    r.w_pad[32:40, :] = jnp.where(iota((8, 64), 0) == 0, jnp.broadcast_to(r.w_in[32:33, :], (8, 64)), first)
    r.w_pad[40:48, :] = jnp.zeros((8, 64), F32)
    r.k_in[...] = hi_hi_lo(dot_tn(r.w_pad[...], repeat_matrix(48, 48, 3), HIGHEST), 48)
    rep = repeat_matrix(64, 64, 3)
    for i in range(2):
        w = r.w_mid[i]
        r.k_mid[i] = hi_hi_lo(dot_full(w, rep), 64)
        r.k_back[i] = hi_hi_lo(dot_tn(w, rep, HIGHEST), 64)
    own = jnp.where(iota((CH, 128), 1) == iota((CH, 128), 0) + chan * CH, 1.0, 0.0)
    w_own = dot_nt(own, r.w_out[...], HIGHEST)
    r.k_out[...] = hi_hi_lo(dot_full(w_own, rep), 64)
    r.k_outback[...] = hi_hi_lo(dot_tn(w_own, repeat_matrix(CH, CH, 4), HIGHEST), CH)
    r.rate_col[...] = jnp.broadcast_to(to_column(r.rate[...], CH, chan * CH), (CH, 128))
    r.bias_col[0] = jnp.broadcast_to(to_column(r.b_mid[0:1, :], 64, 0), (64, 128))
    r.bias_col[1] = jnp.broadcast_to(to_column(r.b_mid[1:2, :], 64, 0), (64, 128))


def wide(block, times):
    return jnp.concatenate([block] * times, axis=1)


def fraction(seq, base):
    pos = seq * TB + base + iota((CH, CHUNK), 1)
    return pos.astype(F32) * (1.0 / L)


def net_forward(r, seq):
    per = CHUNK // 128

    def step(j, carry):
        base = pl.multiple_of(j * CHUNK, CHUNK)
        lanes = pl.ds(base, CHUNK)
        pos = seq * TB + base + iota((48, CHUNK), 1)
        row = iota((48, CHUNK), 0)
        phase = ((wide(r.bands[0], per) * pos + (wide(r.bands[1], per) + L // 2)) & (L - 1)) - L // 2
        phase = jnp.where(phase > L // 4, L // 2 - phase, phase)
        phase = jnp.where(phase < -(L // 4), -(L // 2) - phase, phase)
        wave = sin_small(phase.astype(F32) * (2.0 * math.pi / L))
        frac = pos.astype(F32) * (1.0 / L)
        hi, lo = split(jnp.where(row == 0, frac, jnp.where(row == 33, 1.0, wave)))
        r.feat[0:48, lanes] = hi
        r.feat[48:64, lanes] = jnp.zeros((16, CHUNK), LOW)
        r.feat[64:112, lanes] = lo
        r.feat[112:128, lanes] = jnp.zeros((16, CHUNK), LOW)
        z = low_dot(r.k_in[...], jnp.concatenate([hi, lo, hi], axis=0))
        for layer in range(3):
            s, c = sin_cos(z)
            r.der[layer, :, lanes] = c
            hi, lo = split(s)
            r.act[layer, 0:64, lanes] = hi
            r.act[layer, 64:128, lanes] = lo
            x = jnp.concatenate([hi, lo, hi], axis=0)
            if layer < 2:
                z = low_dot(r.k_mid[layer], x) + wide(r.bias_col[layer], per)
        raw = low_dot(r.k_out[...], x) * jnp.exp(-wide(r.rate_col[...], per) * frac[0:CH, :])
        for i in range(per):
            r.raw_all[seq * ABLK + j * per + i] = raw[:, 128 * i : 128 * i + 128]
        return carry

    lax.fori_loop(0, TB // CHUNK, step, 0)


def net_backward(r, seq):
    per = CHUNK // 128
    r.acc[...] = jnp.zeros_like(r.acc)
    r.acc_out[...] = jnp.zeros_like(r.acc_out)
    r.acc_bias[...] = jnp.zeros_like(r.acc_bias)
    r.acc_rate[...] = jnp.zeros_like(r.acc_rate)

    def lane_sum(x):
        total = x[:, 0:128]
        for i in range(1, per):
            total = total + x[:, 128 * i : 128 * i + 128]
        return total

    def step(j, carry):
        lanes = pl.ds(pl.multiple_of(j * CHUNK, CHUNK), CHUNK)
        start = seq * ABLK + j * per
        grad = jnp.concatenate([r.total[j * per + i] for i in range(per)], axis=1)
        raw = jnp.concatenate([r.raw_all[start + i] for i in range(per)], axis=1)
        frac = fraction(seq, j * CHUNK)
        r.acc_rate[...] -= lane_sum(grad * raw * frac)
        shaped = grad * jnp.exp(-wide(r.rate_col[...], per) * frac)
        hi = shaped.astype(LOW).astype(F32)
        lo = shaped - hi
        pair = jnp.concatenate([hi, lo], axis=0).astype(LOW)
        r.acc_out[...] += dot_nt(pair, r.act[2, :, lanes])
        d = low_dot(r.k_outback[...], jnp.concatenate([hi, lo, hi, jnp.zeros_like(hi)], axis=0).astype(LOW))
        for layer in (2, 1, 0):
            d = d * r.der[layer, :, lanes]
            hi, lo = split(d)
            pair = jnp.concatenate([hi, lo], axis=0)
            if layer:
                r.acc_bias[layer - 1] += lane_sum(d)
                r.acc[layer] += dot_nt(pair, r.act[layer - 1, :, lanes])
                d = low_dot(r.k_back[layer - 1], jnp.concatenate([hi, lo, hi], axis=0))
            else:
                r.acc[0] += dot_nt(pair, r.feat[:, lanes])
        return carry

    lax.fori_loop(0, TB // CHUNK, step, 0)


def fold_halves(x):
    n = x.shape[0] // 2
    total = x[0:n] + x[n:]
    return total + pltpu.roll(total, 64, 1)


def pack_shares(r):
    lane = iota((64, 128), 1)
    r.block[0] = jnp.where(lane < 64, fold_halves(r.acc[1]), fold_halves(r.acc[2]))
    block = fold_halves(r.acc[0])
    block = jnp.where(lane == 34, jnp.sum(r.acc_bias[0], axis=1, keepdims=True), block)
    r.block[1] = jnp.where(lane == 35, jnp.sum(r.acc_bias[1], axis=1, keepdims=True), block)
    lane = iota((CH, 128), 1)
    own = pltpu.roll(fold_halves(r.acc_out[...]), 48, 1)
    own = jnp.where(lane == 112, jnp.sum(r.acc_rate[...], axis=1, keepdims=True), own)
    own = jnp.where(lane == 113, r.skip_part[...], own)

    def place(s, carry):
        rows = pl.ds(pl.multiple_of(8 * s, 8), 8)
        r.share[s, :, 0:128] = r.block[0, rows, :]
        r.share[s, :, 128:256] = jnp.where(lane < 48, r.block[1, rows, :], own)
        return carry

    lax.fori_loop(0, NSEQ, place, 0)


def to_low(x):
    return x.astype(LOW)


def channel_rows(c):
    return pl.ds(c, A, stride=CH)


def forward_pair(r, x):
    tc, ts = r.turn[0], r.turn[1]
    g = low_dot(r.w1[...], x)
    parts = []
    for n in range(2):
        re, im = g[0:A, n * B : n * B + B], g[A:, n * B : n * B + B]
        parts.append(jnp.concatenate([to_low(re * tc + im * ts), to_low(im * tc - re * ts)], axis=1))
    f = low_dot(jnp.concatenate(parts, axis=0), r.fwd[...])
    return f[0:A], f[A:]


def inverse_pair(r, specs):
    tc, ts = r.turn[0], r.turn[1]
    s = jnp.concatenate([jnp.concatenate([to_low(re), to_low(im)], axis=1) for re, im in specs], axis=0)
    t = low_dot(s, r.inv[...])
    cols = []
    for n in range(2):
        re, im = t[n * A : n * A + A, 0:B], t[n * A : n * A + A, B:]
        cols.append(jnp.concatenate([to_low(re * tc - im * ts), to_low(re * ts + im * tc)], axis=0))
    y = low_dot(r.w1t[...], jnp.concatenate(cols, axis=1))
    return y[:, 0:B], y[:, B:]


BLK = 16
VMEM_MAIN = 56 << 20


def gate_products(r, n):
    def step(j, acc):
        part = pl.ds(j * BLK, BLK)
        rows = pl.ds(pl.multiple_of(j * (BLK * CH), BLK * CH), BLK * CH)
        m = r.val[n, part].astype(F32) * r.gin[n, part].astype(F32)
        g = r.cot[n, part].astype(F32) * r.gout[n, part].astype(F32)
        r.mixed[n, rows, :] = m.reshape(BLK * CH, B)
        r.inner[n, rows, :] = g.reshape(BLK * CH, B)
        return acc + jnp.sum(m * g, axis=0)

    return lax.fori_loop(0, A // BLK, step, jnp.zeros((CH, B), F32))


def spectra(r, p):
    cross = []
    for i in range(2):
        c = 2 * p + i
        rows = channel_rows(c)
        fm = forward_pair(r, jnp.concatenate([to_low(r.mixed[n, rows, :]) for n in range(2)], axis=1))
        fg = forward_pair(r, jnp.concatenate([to_low(r.inner[n, rows, :]) for n in range(2)], axis=1))
        re = im = None
        for n in range(2):
            r.f_mixed[c, n] = fm[n]
            r.f_inner[c, n] = fg[n]
            mr, mi = fm[n][:, 0:B], fm[n][:, B:]
            gr, gi = fg[n][:, 0:B], fg[n][:, B:]
            pr, pi = mr * gr + mi * gi, mr * gi - mi * gr
            re, im = (pr, pi) if re is None else (re + pr, im + pi)
        cross.append((re, im))
    ys = inverse_pair(r, cross)
    for i in range(2):
        r.gk[channel_rows(2 * p + i), :] = ys[i]


def normalize(r):
    def rows_of(j):
        return pl.ds(pl.multiple_of(j * (BLK * CH), BLK * CH), BLK * CH)

    def sums(j, carry):
        square, along = carry
        x = r.raw_all[pl.ds(j * BLK, BLK)]
        y = r.gk[rows_of(j), :].reshape(BLK, CH, B)
        return square + jnp.sum(x * x, axis=0), along + jnp.sum(x * y, axis=0)

    zero = jnp.zeros((CH, B), F32)
    square, along = lax.fori_loop(0, A // BLK, sums, (zero, zero))
    norm = jnp.sqrt(jnp.sum(square, axis=1, keepdims=True) + EPSILON)
    along = jnp.sum(along, axis=1, keepdims=True) * (1.0 / L)
    recip = jnp.broadcast_to(1.0 / norm, (CH, B))
    scale_gk = (recip * (1.0 / L))[None]
    scale_raw = jnp.broadcast_to(along / (norm * norm * norm), (CH, B))[None]

    def settle(j, carry):
        part = pl.ds(j * BLK, BLK)
        x = r.raw_all[part]
        r.grad_all[part] = r.gk[rows_of(j), :].reshape(BLK, CH, B) * scale_gk - x * scale_raw
        r.kern[rows_of(j), :] = (x * recip[None]).reshape(BLK * CH, B)
        return carry

    lax.fori_loop(0, A // BLK, settle, 0)


def filter_products(r, p):
    fk = forward_pair(r, jnp.concatenate([to_low(r.kern[channel_rows(2 * p + i), :]) for i in range(2)], axis=1))
    for i in range(2):
        c = 2 * p + i
        rows = channel_rows(c)
        kr, ki = fk[i][:, 0:B] * (1.0 / L), fk[i][:, B:] * (1.0 / L)
        specs = []
        for n in range(2):
            mr, mi = r.f_mixed[c, n, :, 0:B], r.f_mixed[c, n, :, B:]
            specs.append((mr * kr - mi * ki, mr * ki + mi * kr))
        ys = inverse_pair(r, specs)
        for n in range(2):
            r.conv[n, rows, :] = ys[n]
        specs = []
        for n in range(2):
            gr, gi = r.f_inner[c, n, :, 0:B], r.f_inner[c, n, :, B:]
            specs.append((gr * kr + gi * ki, gi * kr - gr * ki))
        ys = inverse_pair(r, specs)
        for n in range(2):
            r.back[n, rows, :] = ys[n]


def finish(r, n):
    gain = jnp.broadcast_to(to_column(r.skip[...], CH, 0), (CH, B))[None]

    def step(j, carry):
        part = pl.ds(j * BLK, BLK)
        rows = pl.ds(pl.multiple_of(j * (BLK * CH), BLK * CH), BLK * CH)
        shape = (BLK, CH, B)
        full = r.conv[n, rows, :].reshape(shape) + gain * r.mixed[n, rows, :].reshape(shape)
        r.o_gout[n, part] = to_low(r.cot[n, part].astype(F32) * full)
        full = r.back[n, rows, :].reshape(shape) + gain * r.inner[n, rows, :].reshape(shape)
        r.o_val[n, part] = to_low(full * r.gin[n, part].astype(F32))
        r.o_gin[n, part] = to_low(full * r.val[n, part].astype(F32))
        return carry

    lax.fori_loop(0, A // BLK, step, 0)


SMALL = ("bands", "w_in", "b_in", "w_mid", "b_mid", "w_out", "rate", "skip")
TABLES = ("w1", "w1t", "fwd", "inv", "turn")
LARGE = ("val", "gin", "cot", "gout")
OUTS = ("o_val", "o_gin", "o_gout", "second", "third", "g_skip")
BIG = (2, A, CH, B)
FULL = (2, A * CH, B)
SCRATCH = {
    "bands": ((2, 48, 128), jnp.int32),
    "w_in": ((33, 64), F32),
    "b_in": ((1, 64), F32),
    "w_mid": ((2, 64, 64), F32),
    "b_mid": ((2, 64), F32),
    "w_out": ((64, 128), F32),
    "rate": ((1, 128), F32),
    "skip": ((1, CH), F32),
    "w1": ((2 * A, A), LOW),
    "w1t": ((A, 2 * A), LOW),
    "fwd": ((2 * B, 2 * B), LOW),
    "inv": ((2 * B, 2 * B), LOW),
    "turn": ((2, A, B), F32),
    "val": (BIG, LOW),
    "gin": (BIG, LOW),
    "cot": (BIG, LOW),
    "gout": (BIG, LOW),
    "w_pad": ((48, 64), F32),
    "k_in": ((64, 144), LOW),
    "k_mid": ((2, 64, 192), LOW),
    "k_back": ((2, 64, 192), LOW),
    "k_out": ((CH, 192), LOW),
    "k_outback": ((64, 4 * CH), LOW),
    "rate_col": ((CH, 128), F32),
    "bias_col": ((2, 64, 128), F32),
    "feat": ((128, TB), LOW),
    "act": ((3, 128, TB), LOW),
    "der": ((3, 64, TB), F32),
    "raw_all": ((A, CH, B), F32),
    "grad_all": ((A, CH, B), F32),
    "total": ((ABLK, CH, B), F32),
    "half": ((2, 2, ABLK // 2, CH, B), F32),
    "side": ((2, 2, ABLK, CH, B), F32),
    "side_out": ((2, 2, ABLK, CH, B), F32),
    "pair": ((2, ABLK, CH, B), F32),
    "mixed": (FULL, F32),
    "inner": (FULL, F32),
    "f_mixed": ((CH, 2, A, 2 * B), F32),
    "f_inner": ((CH, 2, A, 2 * B), F32),
    "gk": ((A * CH, B), F32),
    "kern": ((A * CH, B), F32),
    "conv": (FULL, F32),
    "back": (FULL, F32),
    "acc": ((3, 128, 128), F32),
    "acc_out": ((16, 128), F32),
    "acc_bias": ((2, 64, 128), F32),
    "acc_rate": ((CH, 128), F32),
    "skip_part": ((CH, 1), F32),
    "block": ((2, 64, 128), F32),
    "share": ((NSEQ, 8, 256), F32),
    "first": ((NSEQ, 8, 256), F32),
}
N_LOCAL = len(SMALL) + len(TABLES) + len(LARGE)


def main_kernel(*refs):
    ins = refs[:N_LOCAL]
    outs = refs[N_LOCAL : N_LOCAL + len(OUTS)]
    names = list(SCRATCH)
    scratch = refs[N_LOCAL + len(OUTS) :]
    r = Refs(**dict(zip(OUTS, outs)), **dict(zip(names, scratch)))
    (load_sem, ag_send, ag_recv, rs_send, rs_recv, sem_b, recv_b, sem_c, recv_c, sem_d, recv_d) = scratch[len(names) :]
    chan, seq = lax.axis_index("chan"), lax.axis_index("seq")
    barrier = pltpu.get_barrier_semaphore()

    def signal(device):
        pl.semaphore_signal(barrier, inc=1, device_id=device, device_id_type=MESH)

    def hail_seq(d, carry):
        signal((chan, lax.rem(seq + d, NSEQ)))
        return carry

    def hail_chan(d, carry):
        signal((lax.rem(chan + d, NCHAN), seq))
        return carry

    loads = {}
    for i, name in enumerate(SMALL + TABLES + LARGE):
        loads[name] = pltpu.make_async_copy(ins[i], getattr(r, name), load_sem.at[i])
    for name in SMALL:
        loads[name].start()
    lax.fori_loop(1, NSEQ, hail_seq, 0)
    lax.fori_loop(1, NCHAN, hail_chan, 0)
    for name in LARGE + TABLES:
        loads[name].start()
    for name in SMALL:
        loads[name].wait()

    prepare_weights(r, chan)
    net_forward(r, seq)
    pl.semaphore_wait(barrier, NSEQ - 1 + NCHAN - 1)

    x, z = lax.div(seq, 2), lax.rem(seq, 2)
    xr, xl, xo = lax.rem(x + 1, 4), lax.rem(x + 3, 4), lax.rem(x + 2, 4)
    other = 1 - z
    to_z, to_r, to_l = (chan, 2 * x + other), (chan, 2 * xr + z), (chan, 2 * xl + z)
    HALF = ABLK // 2

    def gather(i, row, count, device):
        part = r.raw_all.at[pl.ds(row, count)]
        return pltpu.make_async_remote_copy(
            src_ref=part, dst_ref=part, send_sem=ag_send.at[i], recv_sem=ag_recv.at[i],
            device_id=device, device_id_type=MESH,
        )

    def row_of(xx, zz):
        return (2 * xx + zz) * ABLK

    ag = [gather(0, row_of(x, z), ABLK, to_z), gather(1, row_of(x, z), ABLK, to_r), gather(2, row_of(x, z), ABLK, to_l)]
    for copy in ag:
        copy.start()

    for name in LARGE:
        loads[name].wait()
    acc = gate_products(r, 0)
    acc = acc + gate_products(r, 1)
    r.skip_part[...] = jnp.sum(acc, axis=1, keepdims=True)

    ag[0].wait_recv()
    ag += [gather(3, row_of(x, other), ABLK, to_r), gather(4, row_of(x, other), ABLK, to_l)]
    ag[3].start()
    ag[4].start()
    ag[1].wait_recv()
    ag += [gather(5, row_of(xl, z), HALF, to_r)]
    ag[5].start()
    ag[2].wait_recv()
    ag += [gather(6, row_of(xr, z) + HALF, HALF, to_l)]
    ag[6].start()
    for name in TABLES:
        loads[name].wait()

    def loop(body, start, stop):
        def step(p, carry):
            body(r, p)
            return carry

        lax.fori_loop(start, stop, step, 0)

    loop(spectra, 0, 3)
    ag[3].wait_recv()
    ag += [gather(7, row_of(xl, other), HALF, to_r)]
    ag[7].start()
    ag[4].wait_recv()
    ag += [gather(8, row_of(xr, other) + HALF, HALF, to_l)]
    ag[8].start()
    loop(spectra, 3, 4)
    for i in (5, 6, 7, 8):
        ag[i].wait_recv()

    normalize(r)

    def send(i, src, dst, device):
        return pltpu.make_async_remote_copy(
            src_ref=src, dst_ref=dst, send_sem=rs_send.at[i], recv_sem=rs_recv.at[i],
            device_id=device, device_id_type=MESH,
        )

    zs = (other, z)
    rs = []
    for w in range(2):
        far = row_of(xo, zs[w])
        rs += [
            send(2 * w, r.grad_all.at[pl.ds(far, HALF)], r.half.at[w, 0], to_r),
            send(2 * w + 1, r.grad_all.at[pl.ds(far + HALF, HALF)], r.half.at[w, 1], to_l),
        ]
    for copy in rs:
        copy.start()

    def add_half(w):
        rs[2 * w].wait_recv()
        near = row_of(xr, zs[w])
        r.side_out[w, 0, 0:HALF] = r.grad_all[pl.ds(near, HALF)] + r.half[w, 0]
        r.side_out[w, 0, HALF:] = r.grad_all[pl.ds(near + HALF, HALF)]
        rs[2 * w + 1].wait_recv()
        near = row_of(xl, zs[w])
        r.side_out[w, 1, 0:HALF] = r.grad_all[pl.ds(near, HALF)]
        r.side_out[w, 1, HALF:] = r.grad_all[pl.ds(near + HALF, HALF)] + r.half[w, 1]
        for i, device in enumerate((to_r, to_l)):
            copy = send(4 + 2 * w + i, r.side_out.at[w, i], r.side.at[w, i], device)
            copy.start()
            rs.append(copy)

    def own_sum(w):
        rs[4 + 2 * w].wait_recv()
        rs[5 + 2 * w].wait_recv()
        return r.grad_all[pl.ds(row_of(x, zs[w]), ABLK)] + r.side[w, 0] + r.side[w, 1]

    loop(filter_products, 0, 1)
    add_half(0)
    loop(filter_products, 1, 2)
    add_half(1)
    loop(filter_products, 2, 4)
    r.pair[0] = own_sum(0)
    rs.append(send(8, r.pair.at[0], r.pair.at[1], to_z))
    rs[8].start()
    r.total[...] = own_sum(1)
    finish(r, 0)
    rs[8].wait_recv()
    r.total[...] += r.pair[1]
    for copy in ag + rs:
        copy.wait_send()

    net_backward(r, seq)
    pack_shares(r)

    def run(size, make):
        def start(d, carry):
            make(d).start()
            return carry

        def wait(d, carry):
            make(d).wait()
            return carry

        lax.fori_loop(1, size, start, 0)
        return lambda: lax.fori_loop(1, size, wait, 0)

    def seq_peer(d):
        return (chan, lax.rem(seq + d, NSEQ))

    def make_b(d):
        return pltpu.make_async_remote_copy(
            src_ref=r.share.at[lax.rem(seq + d, NSEQ)], dst_ref=r.first.at[d],
            send_sem=sem_b.at[d], recv_sem=recv_b.at[d], device_id=seq_peer(d), device_id_type=MESH,
        )

    def make_c(d):
        return pltpu.make_async_remote_copy(
            src_ref=r.second.at[chan], dst_ref=r.second.at[chan], send_sem=sem_c.at[d], recv_sem=recv_c.at[d],
            device_id=(lax.rem(chan + d, NCHAN), seq), device_id_type=MESH,
        )

    def make_d(d):
        return pltpu.make_async_remote_copy(
            src_ref=r.third.at[seq], dst_ref=r.third.at[seq], send_sem=sem_d.at[d], recv_sem=recv_d.at[d],
            device_id=seq_peer(d), device_id_type=MESH,
        )

    wait = run(NSEQ, make_b)
    finish(r, 1)
    wait()
    total = r.share[seq]
    for d in range(1, NSEQ):
        total = total + r.first[d]
    factor = 1.0 / math.sqrt(16 * L)
    total = total * factor
    r.second[chan] = total
    r.g_skip[...] = to_row(total[:, 241:242])
    run(NCHAN, make_c)()
    total = r.second[0]
    for c in range(1, NCHAN):
        total = total + r.second[c]
    r.third[seq] = total
    run(NSEQ, make_d)()


def write_kernel(
    i_val, i_gin, i_gout, second, third, skip,
    o_val, o_gin, o_gout, g_skip, g_in, g_bin, g_mid, g_bmid, g_out, g_rate, sems,
):
    copies = [
        pltpu.make_async_copy(src, dst, sems.at[i])
        for i, (src, dst) in enumerate(((i_val, o_val), (i_gin, o_gin), (i_gout, o_gout)))
    ]
    for copy in copies:
        copy.start()
    g_skip[...] = skip[...]
    hidden = third[...].reshape(64, 256)
    g_mid[0] = hidden[:, 0:64]
    g_mid[1] = pltpu.roll(hidden[:, 0:128], 64, 1)[:, 0:64]
    flat = jnp.transpose(hidden[:, 128:256])
    g_in[...] = flat[0:33, :]
    g_bin[...] = flat[33:34, :]
    g_bmid[...] = flat[34:36, :]
    own = jnp.transpose(second[...].reshape(128, 256)[:, 128:256])
    g_out[...] = own[48:112, :]
    g_rate[...] = own[112:113, :]
    for copy in copies:
        copy.wait()


def sds(shape, dtype=F32):
    return jax.ShapeDtypeStruct(shape, dtype)


VM = pl.BlockSpec(memory_space=pltpu.VMEM)
HB = pl.BlockSpec(memory_space=pl.ANY)
DMA = pltpu.SemaphoreType.DMA


def to_natural(x):
    return x.reshape(2, CH, A, B).transpose(0, 2, 1, 3)


def from_natural(x):
    return x.transpose(0, 2, 1, 3).reshape(2, CH, L)


def local(
    value, gate_in, gate_out, cotangent, skip_gain,
    weight_in, bias_in, weight_mid, bias_mid, weight_out, decay_rate,
):
    small = (
        row_constants(), weight_in.T, bias_in.reshape(1, 64), weight_mid, bias_mid, weight_out.T,
        decay_rate.reshape(1, 128), skip_gain.reshape(1, CH),
    )
    large = tuple(to_natural(x) for x in (value, gate_in, cotangent, gate_out))
    big = sds(BIG, LOW)
    o_val, o_gin, o_gout, second, third, g_skip = pl.pallas_call(
        main_kernel,
        out_shape=[big, big, big, sds((NCHAN, 8, 256)), sds((NSEQ, 8, 256)), sds((1, CH))],
        in_specs=[HB] * N_LOCAL,
        out_specs=[VM] * len(OUTS),
        scratch_shapes=[pltpu.VMEM(shape, dtype) for shape, dtype in SCRATCH.values()]
        + [
            DMA((N_LOCAL,)), DMA((9,)), DMA((9,)), DMA((9,)), DMA((9,)),
            DMA((NSEQ,)), DMA((NSEQ,)), DMA((NCHAN,)), DMA((NCHAN,)), DMA((NSEQ,)), DMA((NSEQ,)),
        ],
        compiler_params=pltpu.CompilerParams(
            collective_id=0, has_side_effects=True, vmem_limit_bytes=VMEM_MAIN
        ),
        name="hyena_backward",
    )(*small, *transform_tables(), *large)
    o_val, o_gin, o_gout, g_skip, g_in, g_bin, g_mid, g_bmid, g_out, g_rate = pl.pallas_call(
        write_kernel,
        out_shape=[
            big, big, big, sds((1, CH)), sds((33, 64)), sds((1, 64)), sds((2, 64, 64)), sds((2, 64)),
            sds((64, 128)), sds((1, 128)),
        ],
        in_specs=[HB] * 3 + [VM] * 3,
        out_specs=[HB] * 3 + [VM] * 7,
        scratch_shapes=[DMA((3,))],
        name="write_results",
    )(o_val, o_gin, o_gout, second, third, g_skip)
    return (
        from_natural(o_val), from_natural(o_gin), from_natural(o_gout), g_skip.reshape(CH),
        g_in.T, g_bin.reshape(64), g_mid, g_bmid, g_out.T, g_rate.reshape(128),
    )


def solution(mesh):
    return jax.shard_map(
        local,
        mesh=mesh,
        in_specs=(
            P("seq", "chan", None), P("seq", "chan", None), P("seq", "chan", None), P("seq", "chan", None),
            P("chan"), P(), P(), P(), P(), P(), P(),
        ),
        out_specs=(
            P("seq", "chan", None), P("seq", "chan", None), P("seq", "chan", None),
            P("chan"), P(), P(), P(), P(), P(), P(),
        ),
        check_vma=False,
    )
```

profile of v0, /device:TPU:1, one launch (start us, length us, event | category | flops | bytes accessed | tf_op | source)
XLA Modules:
  0.0 159.2 jit_solution(13631854998184216996)
XLA Ops:
  0.6 60.5 %hyena_backward.1 = (bf16[2,256,8,128]{3,2,1,0:T(8,128)(2,1)}, bf16[2,256,8,128]{3,2,1,0:T(8,128)(2,1)}, bf16[2,256,8,128]{3,2,1,0:T(8,128)(2,1)}, f32[16,8,256]...) custom-call(s32[2,48,128]{2,1,0:T(8,128)} %constant.12.clone.refs_0_, f32[33,64]{1,0:T(8,128)} %bitcast.36, ...), custom_call_target="tpu_custom_call" | custom-call | tf_op jit(solution)/shard_map/hyena_backward/pallas_call | solution.py:738
  61.2 98.0 %write_results.1 = (bf16[2,256,8,128]{3,2,1,0:T(8,128)(2,1)}, bf16[2,256,8,128]{3,2,1,0:T(8,128)(2,1)}, bf16[2,256,8,128]{3,2,1,0:T(8,128)(2,1)}, f32[1,8]{1,0:T...) custom-call(bf16[2,256,8,128]{3,2,1,0:T(8,128)(2,1)} %get-tuple-elem, ...), custom_call_target="tpu_custom_call" | custom-call | tf_op jit(solution)/shard_map/write_results/pallas_call | solution.py:753
where the time goes:
time: 159 us
  Pallas kernels  159 us (100%)
    pallas_call x1, Pallas kernels, local(): pl.pallas_call(write_kernel, out_shape=[big, big, big, sds((1, CH)), sds(...  98 us
    pallas_call x1, Pallas kernels, local(): pl.pallas_call(main_kernel, out_shape=[big, big, big, sds((NCHAN, 8, 256)...  60.5 us

commit v1 on v0

--- a/solution.py
+++ b/solution.py
@@ -423,7 +423,7 @@
 SMALL = ("bands", "w_in", "b_in", "w_mid", "b_mid", "w_out", "rate", "skip")
 TABLES = ("w1", "w1t", "fwd", "inv", "turn")
 LARGE = ("val", "gin", "cot", "gout")
-OUTS = ("o_val", "o_gin", "o_gout", "second", "third", "g_skip")
+OUTS = ("h_val", "h_gin", "h_gout", "second", "third", "g_skip")
 BIG = (2, A, CH, B)
 FULL = (2, A * CH, B)
 SCRATCH = {
@@ -444,6 +444,9 @@
     "gin": (BIG, LOW),
     "cot": (BIG, LOW),
     "gout": (BIG, LOW),
+    "o_val": (BIG, LOW),
+    "o_gin": (BIG, LOW),
+    "o_gout": (BIG, LOW),
     "w_pad": ((48, 64), F32),
     "k_in": ((64, 144), LOW),
     "k_mid": ((2, 64, 192), LOW),
@@ -488,7 +491,7 @@
     names = list(SCRATCH)
     scratch = refs[N_LOCAL + len(OUTS) :]
     r = Refs(**dict(zip(OUTS, outs)), **dict(zip(names, scratch)))
-    (load_sem, ag_send, ag_recv, rs_send, rs_recv, sem_b, recv_b, sem_c, recv_c, sem_d, recv_d) = scratch[len(names) :]
+    (load_sem, out_sem, ag_send, ag_recv, rs_send, rs_recv, sem_b, recv_b, sem_c, recv_c, sem_d, recv_d) = scratch[len(names) :]
     chan, seq = lax.axis_index("chan"), lax.axis_index("seq")
     barrier = pltpu.get_barrier_semaphore()
 
@@ -624,6 +627,15 @@
     rs[8].start()
     r.total[...] = own_sum(1)
     finish(r, 0)
+    results = []
+
+    def leave(n):
+        for i, (src, dst) in enumerate(((r.o_val, r.h_val), (r.o_gin, r.h_gin), (r.o_gout, r.h_gout))):
+            copy = pltpu.make_async_copy(src.at[n], dst.at[n], out_sem.at[3 * n + i])
+            copy.start()
+            results.append(copy)
+
+    leave(0)
     rs[8].wait_recv()
     r.total[...] += r.pair[1]
     for copy in ag + rs:
@@ -667,6 +679,7 @@
 
     wait = run(NSEQ, make_b)
     finish(r, 1)
+    leave(1)
     wait()
     total = r.share[seq]
     for d in range(1, NSEQ):
@@ -681,19 +694,32 @@
         total = total + r.second[c]
     r.third[seq] = total
     run(NSEQ, make_d)()
+    for copy in results:
+        copy.wait()
 
 
 def write_kernel(
-    i_val, i_gin, i_gout, second, third, skip,
-    o_val, o_gin, o_gout, g_skip, g_in, g_bin, g_mid, g_bmid, g_out, g_rate, sems,
+    i_val, i_gin, i_gout, i_second, i_third, skip,
+    o_val, o_gin, o_gout, g_skip, g_in, g_bin, g_mid, g_bmid, g_out, g_rate,
+    stage, second, third, in_sem, out_sem, small_sem,
 ):
-    copies = [
-        pltpu.make_async_copy(src, dst, sems.at[i])
-        for i, (src, dst) in enumerate(((i_val, o_val), (i_gin, o_gin), (i_gout, o_gout)))
+    loads, stores = [], []
+    for i, (src, dst) in enumerate(((i_val, o_val), (i_gin, o_gin), (i_gout, o_gout))):
+        for n in range(2):
+            loads.append(pltpu.make_async_copy(src.at[n], stage.at[i, n], in_sem.at[2 * i + n]))
+            stores.append(pltpu.make_async_copy(stage.at[i, n], dst.at[n], out_sem.at[2 * i + n]))
+    small = [
+        pltpu.make_async_copy(i_second, second, small_sem.at[0]),
+        pltpu.make_async_copy(i_third, third, small_sem.at[1]),
     ]
-    for copy in copies:
+    for copy in small + loads:
         copy.start()
     g_skip[...] = skip[...]
+    for load, store in zip(loads, stores):
+        load.wait()
+        store.start()
+    for copy in small:
+        copy.wait()
     hidden = third[...].reshape(64, 256)
     g_mid[0] = hidden[:, 0:64]
     g_mid[1] = pltpu.roll(hidden[:, 0:128], 64, 1)[:, 0:64]
@@ -704,7 +730,7 @@
     own = jnp.transpose(second[...].reshape(128, 256)[:, 128:256])
     g_out[...] = own[48:112, :]
     g_rate[...] = own[112:113, :]
-    for copy in copies:
+    for copy in stores:
         copy.wait()
 
 
@@ -713,7 +739,7 @@
 
 
 VM = pl.BlockSpec(memory_space=pltpu.VMEM)
-HB = pl.BlockSpec(memory_space=pl.ANY)
+HB = pl.BlockSpec(memory_space=pltpu.HBM)
 DMA = pltpu.SemaphoreType.DMA
 
 
@@ -739,10 +765,10 @@
         main_kernel,
         out_shape=[big, big, big, sds((NCHAN, 8, 256)), sds((NSEQ, 8, 256)), sds((1, CH))],
         in_specs=[HB] * N_LOCAL,
-        out_specs=[VM] * len(OUTS),
+        out_specs=[HB] * 3 + [VM] * 3,
         scratch_shapes=[pltpu.VMEM(shape, dtype) for shape, dtype in SCRATCH.values()]
         + [
-            DMA((N_LOCAL,)), DMA((9,)), DMA((9,)), DMA((9,)), DMA((9,)),
+            DMA((N_LOCAL,)), DMA((6,)), DMA((9,)), DMA((9,)), DMA((9,)), DMA((9,)),
             DMA((NSEQ,)), DMA((NSEQ,)), DMA((NCHAN,)), DMA((NCHAN,)), DMA((NSEQ,)), DMA((NSEQ,)),
         ],
         compiler_params=pltpu.CompilerParams(
@@ -756,9 +782,13 @@
             big, big, big, sds((1, CH)), sds((33, 64)), sds((1, 64)), sds((2, 64, 64)), sds((2, 64)),
             sds((64, 128)), sds((1, 128)),
         ],
-        in_specs=[HB] * 3 + [VM] * 3,
+        in_specs=[HB] * 5 + [VM],
         out_specs=[HB] * 3 + [VM] * 7,
-        scratch_shapes=[DMA((3,))],
+        scratch_shapes=[
+            pltpu.VMEM((3,) + BIG, LOW), pltpu.VMEM((NCHAN, 8, 256), F32), pltpu.VMEM((NSEQ, 8, 256), F32),
+            DMA((6,)), DMA((6,)), DMA((2,)),
+        ],
+        compiler_params=pltpu.CompilerParams(vmem_limit_bytes=VMEM_MAIN),
         name="write_results",
     )(o_val, o_gin, o_gout, second, third, g_skip)
     return (

time: 159 us -> 64.4 us (0.41)
  Pallas kernels: 159 us -> 63.6 us
    pallas_call x1, Pallas kernels: 98 us -> 4.08 us  [local(): pl.pallas_call(write_kernel, out_shape=[big, big, big, sds((1, CH)), sds(...]
where the time goes in v1:
time: 64.4 us; the launch traced here: 64.2 us
  Pallas kernels  63.6 us (99%)
  between operations  0.66 us (1%)
    pallas_call x1, Pallas kernels, local(): pl.pallas_call(main_kernel, out_shape=[big, big, big, sds((NCHAN, 8, 256)...  59.5 us
    pallas_call x1, Pallas kernels, local(): pl.pallas_call(write_kernel, out_shape=[big, big, big, sds((1, CH)), sds(...  4.08 us

profile of v1, /device:TPU:1, one launch (start us, length us, event | category | flops | bytes accessed | tf_op | source)
XLA Modules:
  0.0 64.2 jit_solution(7478828299213598389)
XLA Ops:
  0.6 59.5 %hyena_backward.1 = (bf16[2,256,8,128]{3,2,1,0:T(8,128)(2,1)}, bf16[2,256,8,128]{3,2,1,0:T(8,128)(2,1)}, bf16[2,256,8,128]{3,2,1,0:T(8,128)(2,1)}, f32[16,8,256]...) custom-call(s32[2,48,128]{2,1,0:T(8,128)} %constant.12.clone.refs_0_, f32[33,64]{1,0:T(8,128)} %bitcast.36, ...), custom_call_target="tpu_custom_call" | custom-call | tf_op jit(solution)/shard_map/hyena_backward/pallas_call | solution.py:764
  60.1 4.1 %write_results.1 = (bf16[2,256,8,128]{3,2,1,0:T(8,128)(2,1)}, bf16[2,256,8,128]{3,2,1,0:T(8,128)(2,1)}, bf16[2,256,8,128]{3,2,1,0:T(8,128)(2,1)}, f32[1,8]{1,0:T...) custom-call(bf16[2,256,8,128]{3,2,1,0:T(8,128)(2,1)} %get-tuple-elem, ...), custom_call_target="tpu_custom_call" | custom-call | tf_op jit(solution)/shard_map/write_results/pallas_call | solution.py:779

commit v2 on v1

--- a/solution.py
+++ b/solution.py
@@ -181,7 +181,7 @@
     return pos.astype(F32) * (1.0 / L)
 
 
-def net_forward(r, seq):
+def net_forward(r, seq, send):
     per = CHUNK // 128
 
     def step(j, carry):
@@ -212,12 +212,13 @@
         raw = low_dot(r.k_out[...], x) * jnp.exp(-wide(r.rate_col[...], per) * frac[0:CH, :])
         for i in range(per):
             r.raw_all[seq * ABLK + j * per + i] = raw[:, 128 * i : 128 * i + 128]
+        send(j)
         return carry
 
     lax.fori_loop(0, TB // CHUNK, step, 0)
 
 
-def net_backward(r, seq):
+def net_backward(r, seq, scale_gk, scale_raw):
     per = CHUNK // 128
     r.acc[...] = jnp.zeros_like(r.acc)
     r.acc_out[...] = jnp.zeros_like(r.acc_out)
@@ -233,8 +234,9 @@
     def step(j, carry):
         lanes = pl.ds(pl.multiple_of(j * CHUNK, CHUNK), CHUNK)
         start = seq * ABLK + j * per
-        grad = jnp.concatenate([r.total[j * per + i] for i in range(per)], axis=1)
+        grad = jnp.concatenate([r.total[pl.ds(j * per + i, CH, stride=ABLK), :] for i in range(per)], axis=1)
         raw = jnp.concatenate([r.raw_all[start + i] for i in range(per)], axis=1)
+        grad = grad * wide(scale_gk, per) - raw * wide(scale_raw, per)
         frac = fraction(seq, j * CHUNK)
         r.acc_rate[...] -= lane_sum(grad * raw * frac)
         shaped = grad * jnp.exp(-wide(r.rate_col[...], per) * frac)
@@ -350,39 +352,20 @@
         cross.append((re, im))
     ys = inverse_pair(r, cross)
     for i in range(2):
-        r.gk[channel_rows(2 * p + i), :] = ys[i]
-
-
-def normalize(r):
-    def rows_of(j):
-        return pl.ds(pl.multiple_of(j * (BLK * CH), BLK * CH), BLK * CH)
-
-    def sums(j, carry):
-        square, along = carry
-        x = r.raw_all[pl.ds(j * BLK, BLK)]
-        y = r.gk[rows_of(j), :].reshape(BLK, CH, B)
-        return square + jnp.sum(x * x, axis=0), along + jnp.sum(x * y, axis=0)
-
-    zero = jnp.zeros((CH, B), F32)
-    square, along = lax.fori_loop(0, A // BLK, sums, (zero, zero))
-    norm = jnp.sqrt(jnp.sum(square, axis=1, keepdims=True) + EPSILON)
-    along = jnp.sum(along, axis=1, keepdims=True) * (1.0 / L)
-    recip = jnp.broadcast_to(1.0 / norm, (CH, B))
-    scale_gk = (recip * (1.0 / L))[None]
-    scale_raw = jnp.broadcast_to(along / (norm * norm * norm), (CH, B))[None]
-
-    def settle(j, carry):
-        part = pl.ds(j * BLK, BLK)
-        x = r.raw_all[part]
-        r.grad_all[part] = r.gk[rows_of(j), :].reshape(BLK, CH, B) * scale_gk - x * scale_raw
-        r.kern[rows_of(j), :] = (x * recip[None]).reshape(BLK * CH, B)
-        return carry
-
-    lax.fori_loop(0, A // BLK, settle, 0)
+        r.gk[2 * p + i] = ys[i]
 
 
 def filter_products(r, p):
-    fk = forward_pair(r, jnp.concatenate([to_low(r.kern[channel_rows(2 * p + i), :]) for i in range(2)], axis=1))
+    kernels = []
+    for i in range(2):
+        c = 2 * p + i
+        x = r.raw_flat[channel_rows(c), :]
+        square = jnp.sum(x * x, axis=0, keepdims=True)
+        r.stat[0, pl.ds(c, 1), :] = square
+        r.stat[1, pl.ds(c, 1), :] = jnp.sum(x * r.gk[c], axis=0, keepdims=True)
+        norm = jnp.sqrt(jnp.sum(square, axis=1, keepdims=True) + EPSILON)
+        kernels.append(to_low(x / norm))
+    fk = forward_pair(r, jnp.concatenate(kernels, axis=1))
     for i in range(2):
         c = 2 * p + i
         rows = channel_rows(c)
@@ -459,18 +442,17 @@
     "act": ((3, 128, TB), LOW),
     "der": ((3, 64, TB), F32),
     "raw_all": ((A, CH, B), F32),
-    "grad_all": ((A, CH, B), F32),
-    "total": ((ABLK, CH, B), F32),
-    "half": ((2, 2, ABLK // 2, CH, B), F32),
-    "side": ((2, 2, ABLK, CH, B), F32),
-    "side_out": ((2, 2, ABLK, CH, B), F32),
-    "pair": ((2, ABLK, CH, B), F32),
+    "total": ((CH * ABLK, B), F32),
+    "half": ((CH // 2, 2, 2, 2, ABLK // 2, B), F32),
+    "side_out": ((CH // 2, 2, 2, 2, ABLK, B), F32),
+    "side": ((CH // 2, 5, 2, ABLK, B), F32),
+    "stat": ((2, CH, B), F32),
+    "along": ((NSEQ, CH, B), F32),
     "mixed": (FULL, F32),
     "inner": (FULL, F32),
     "f_mixed": ((CH, 2, A, 2 * B), F32),
     "f_inner": ((CH, 2, A, 2 * B), F32),
-    "gk": ((A * CH, B), F32),
-    "kern": ((A * CH, B), F32),
+    "gk": ((CH, A, B), F32),
     "conv": (FULL, F32),
     "back": (FULL, F32),
     "acc": ((3, 128, 128), F32),
@@ -491,7 +473,9 @@
     names = list(SCRATCH)
     scratch = refs[N_LOCAL + len(OUTS) :]
     r = Refs(**dict(zip(OUTS, outs)), **dict(zip(names, scratch)))
-    (load_sem, out_sem, ag_send, ag_recv, rs_send, rs_recv, sem_b, recv_b, sem_c, recv_c, sem_d, recv_d) = scratch[len(names) :]
+    (load_sem, out_sem, ag_send, ag_recv, relay_send, relay_recv, half_send, half_recv, rs_send, rs_recv,
+     sem_a, recv_a, sem_b, recv_b, sem_c, recv_c, sem_d, recv_d) = scratch[len(names) :]
+    r.raw_flat = r.raw_all.reshape(A * CH, B)
     chan, seq = lax.axis_index("chan"), lax.axis_index("seq")
     barrier = pltpu.get_barrier_semaphore()
 
@@ -518,115 +502,152 @@
     for name in SMALL:
         loads[name].wait()
 
-    prepare_weights(r, chan)
-    net_forward(r, seq)
-    pl.semaphore_wait(barrier, NSEQ - 1 + NCHAN - 1)
-
     x, z = lax.div(seq, 2), lax.rem(seq, 2)
     xr, xl, xo = lax.rem(x + 1, 4), lax.rem(x + 3, 4), lax.rem(x + 2, 4)
     other = 1 - z
-    to_z, to_r, to_l = (chan, 2 * x + other), (chan, 2 * xr + z), (chan, 2 * xl + z)
-    HALF = ABLK // 2
-
-    def gather(i, row, count, device):
-        part = r.raw_all.at[pl.ds(row, count)]
-        return pltpu.make_async_remote_copy(
-            src_ref=part, dst_ref=part, send_sem=ag_send.at[i], recv_sem=ag_recv.at[i],
-            device_id=device, device_id_type=MESH,
-        )
+    near = (
+        (chan, 2 * x + other), (chan, 2 * xr + z), (chan, 2 * xr + other), (chan, 2 * xl + z), (chan, 2 * xl + other)
+    )
+    to_r, to_l = near[1], near[3]
+    half = ABLK // 2
+    piece = CHUNK // 128
+    n_piece = ABLK // piece
 
     def row_of(xx, zz):
         return (2 * xx + zz) * ABLK
 
-    ag = [gather(0, row_of(x, z), ABLK, to_z), gather(1, row_of(x, z), ABLK, to_r), gather(2, row_of(x, z), ABLK, to_l)]
-    for copy in ag:
-        copy.start()
+    def gather(i, j):
+        part = r.raw_all.at[pl.ds(row_of(x, z) + j * piece, piece)]
+        return pltpu.make_async_remote_copy(
+            src_ref=part, dst_ref=part, send_sem=ag_send.at[i, j], recv_sem=ag_recv.at[i, j],
+            device_id=near[i], device_id_type=MESH,
+        )
+
+    def send_chunk(j):
+        for i in range(5):
+            gather(i, j).start()
+
+    def relay(i):
+        row = row_of(xl if i < 2 else xr, (z, other)[i % 2]) + (0 if i < 2 else half)
+        part = r.raw_all.at[pl.ds(row, half)]
+        return pltpu.make_async_remote_copy(
+            src_ref=part, dst_ref=part, send_sem=relay_send.at[i], recv_sem=relay_recv.at[i],
+            device_id=to_r if i < 2 else to_l, device_id_type=MESH,
+        )
+
+    def arrived(i, start, stop):
+        def step(j, carry):
+            gather(i, j).wait_recv()
+            return carry
+
+        lax.fori_loop(start, stop, step, 0)
+
+    zs = (other, z)
+
+    def rows_at(p, row, count):
+        return r.gk.at[pl.ds(2 * p, 2), pl.ds(pl.multiple_of(row, half), count)]
+
+    def far_half(p, w, h):
+        return pltpu.make_async_remote_copy(
+            src_ref=rows_at(p, row_of(xo, zs[w]) + h * half, half), dst_ref=r.half.at[p, w, h],
+            send_sem=half_send.at[p, 2 * w + h], recv_sem=half_recv.at[p, 2 * w + h],
+            device_id=(to_r, to_l)[h], device_id_type=MESH,
+        )
+
+    def near_block(p, i):
+        w = i % 2
+        src = rows_at(p, row_of(x, other), ABLK) if i == 0 else r.side_out.at[p, w, (i - 1) // 2]
+        return pltpu.make_async_remote_copy(
+            src_ref=src, dst_ref=r.side.at[p, i], send_sem=rs_send.at[p, i], recv_sem=rs_recv.at[p, i],
+            device_id=near[i], device_id_type=MESH,
+        )
+
+    def scatter_far(p):
+        for w in range(2):
+            for h in range(2):
+                far_half(p, w, h).start()
+        near_block(p, 0).start()
+
+    def scatter_near(p):
+        for w in range(2):
+            for h in range(2):
+                far_half(p, w, h).wait_recv()
+                row = row_of((xr, xl)[h], zs[w])
+                for i in range(2):
+                    mine = r.gk[2 * p + i, pl.ds(pl.multiple_of(row, half), half), :]
+                    rest = r.gk[2 * p + i, pl.ds(pl.multiple_of(row + half, half), half), :]
+                    extra = r.half[p, w, h, i]
+                    r.side_out[p, w, h, i, 0:half, :] = mine + extra if h == 0 else mine
+                    r.side_out[p, w, h, i, half:, :] = rest if h == 0 else rest + extra
+        for i in range(1, 5):
+            near_block(p, i).start()
+
+    prepare_weights(r, chan)
+    pl.semaphore_wait(barrier, NSEQ - 1 + NCHAN - 1)
+    net_forward(r, seq, send_chunk)
 
     for name in LARGE:
         loads[name].wait()
     acc = gate_products(r, 0)
     acc = acc + gate_products(r, 1)
     r.skip_part[...] = jnp.sum(acc, axis=1, keepdims=True)
-
-    ag[0].wait_recv()
-    ag += [gather(3, row_of(x, other), ABLK, to_r), gather(4, row_of(x, other), ABLK, to_l)]
-    ag[3].start()
-    ag[4].start()
-    ag[1].wait_recv()
-    ag += [gather(5, row_of(xl, z), HALF, to_r)]
-    ag[5].start()
-    ag[2].wait_recv()
-    ag += [gather(6, row_of(xr, z) + HALF, HALF, to_l)]
-    ag[6].start()
     for name in TABLES:
         loads[name].wait()
-
-    def loop(body, start, stop):
-        def step(p, carry):
-            body(r, p)
+    for i in range(2):
+        arrived(1 + i, 0, n_piece // 2)
+        relay(i).start()
+
+    spectra(r, 0)
+    scatter_far(0)
+    for i in range(2):
+        arrived(3 + i, n_piece // 2, n_piece)
+        relay(2 + i).start()
+
+    def pair_step(p, carry):
+        spectra(r, p)
+        scatter_far(p)
+        scatter_near(p - 1)
+        return carry
+
+    lax.fori_loop(1, CH // 2, pair_step, 0)
+    arrived(0, 0, n_piece)
+    for i in range(2):
+        arrived(1 + i, n_piece // 2, n_piece)
+        arrived(3 + i, 0, n_piece // 2)
+    for i in range(4):
+        relay(i).wait_recv()
+
+    filter_products(r, 0)
+    scatter_near(CH // 2 - 1)
+
+    def product_step(p, carry):
+        filter_products(r, p)
+        return carry
+
+    lax.fori_loop(1, CH // 2, product_step, 0)
+
+    def run(size, make):
+        def start(d, carry):
+            make(d).start()
             return carry
 
-        lax.fori_loop(start, stop, step, 0)
-
-    loop(spectra, 0, 3)
-    ag[3].wait_recv()
-    ag += [gather(7, row_of(xl, other), HALF, to_r)]
-    ag[7].start()
-    ag[4].wait_recv()
-    ag += [gather(8, row_of(xr, other) + HALF, HALF, to_l)]
-    ag[8].start()
-    loop(spectra, 3, 4)
-    for i in (5, 6, 7, 8):
-        ag[i].wait_recv()
-
-    normalize(r)
-
-    def send(i, src, dst, device):
+        def wait(d, carry):
+            make(d).wait()
+            return carry
+
+        lax.fori_loop(1, size, start, 0)
+        return lambda: lax.fori_loop(1, size, wait, 0)
+
+    def seq_peer(d):
+        return (chan, lax.rem(seq + d, NSEQ))
+
+    def make_a(d):
         return pltpu.make_async_remote_copy(
-            src_ref=src, dst_ref=dst, send_sem=rs_send.at[i], recv_sem=rs_recv.at[i],
-            device_id=device, device_id_type=MESH,
+            src_ref=r.stat.at[1], dst_ref=r.along.at[d],
+            send_sem=sem_a.at[d], recv_sem=recv_a.at[d], device_id=seq_peer(d), device_id_type=MESH,
         )
 
-    zs = (other, z)
-    rs = []
-    for w in range(2):
-        far = row_of(xo, zs[w])
-        rs += [
-            send(2 * w, r.grad_all.at[pl.ds(far, HALF)], r.half.at[w, 0], to_r),
-            send(2 * w + 1, r.grad_all.at[pl.ds(far + HALF, HALF)], r.half.at[w, 1], to_l),
-        ]
-    for copy in rs:
-        copy.start()
-
-    def add_half(w):
-        rs[2 * w].wait_recv()
-        near = row_of(xr, zs[w])
-        r.side_out[w, 0, 0:HALF] = r.grad_all[pl.ds(near, HALF)] + r.half[w, 0]
-        r.side_out[w, 0, HALF:] = r.grad_all[pl.ds(near + HALF, HALF)]
-        rs[2 * w + 1].wait_recv()
-        near = row_of(xl, zs[w])
-        r.side_out[w, 1, 0:HALF] = r.grad_all[pl.ds(near, HALF)]
-        r.side_out[w, 1, HALF:] = r.grad_all[pl.ds(near + HALF, HALF)] + r.half[w, 1]
-        for i, device in enumerate((to_r, to_l)):
-            copy = send(4 + 2 * w + i, r.side_out.at[w, i], r.side.at[w, i], device)
-            copy.start()
-            rs.append(copy)
-
-    def own_sum(w):
-        rs[4 + 2 * w].wait_recv()
-        rs[5 + 2 * w].wait_recv()
-        return r.grad_all[pl.ds(row_of(x, zs[w]), ABLK)] + r.side[w, 0] + r.side[w, 1]
-
-    loop(filter_products, 0, 1)
-    add_half(0)
-    loop(filter_products, 1, 2)
-    add_half(1)
-    loop(filter_products, 2, 4)
-    r.pair[0] = own_sum(0)
-    rs.append(send(8, r.pair.at[0], r.pair.at[1], to_z))
-    rs[8].start()
-    r.total[...] = own_sum(1)
-    finish(r, 0)
+    wait_along = run(NSEQ, make_a)
     results = []
 
     def leave(n):
@@ -635,29 +656,41 @@
             copy.start()
             results.append(copy)
 
+    finish(r, 0)
     leave(0)
-    rs[8].wait_recv()
-    r.total[...] += r.pair[1]
-    for copy in ag + rs:
-        copy.wait_send()
-
-    net_backward(r, seq)
+
+    def settle(p, carry):
+        for i in range(5):
+            near_block(p, i).wait_recv()
+        row = pl.multiple_of(row_of(x, z), ABLK)
+        for i in range(2):
+            c = 2 * p + i
+            total = r.gk[c, pl.ds(row, ABLK), :]
+            for k in range(5):
+                total = total + r.side[p, k, i]
+            r.total[pl.ds(pl.multiple_of(c * ABLK, ABLK), ABLK), :] = total
+        return carry
+
+    lax.fori_loop(0, CH // 2, settle, 0)
+    wait_along()
+    along = r.stat[1]
+    for d in range(1, NSEQ):
+        along = along + r.along[d]
+    along = jnp.sum(along, axis=1, keepdims=True) * (1.0 / L)
+    norm = jnp.sqrt(jnp.sum(r.stat[0], axis=1, keepdims=True) + EPSILON)
+    scale_gk = jnp.broadcast_to((1.0 / L) / norm, (CH, B))
+    scale_raw = jnp.broadcast_to(along / (norm * norm * norm), (CH, B))
+
+    def sent(j, carry):
+        for i in range(5):
+            gather(i, j).wait_send()
+            near_block(j, i).wait_send()
+        for i in range(4):
+            far_half(j, i // 2, i % 2).wait_send()
+        return carry
+
+    net_backward(r, seq, scale_gk, scale_raw)
     pack_shares(r)
-
-    def run(size, make):
-        def start(d, carry):
-            make(d).start()
-            return carry
-
-        def wait(d, carry):
-            make(d).wait()
-            return carry
-
-        lax.fori_loop(1, size, start, 0)
-        return lambda: lax.fori_loop(1, size, wait, 0)
-
-    def seq_peer(d):
-        return (chan, lax.rem(seq + d, NSEQ))
 
     def make_b(d):
         return pltpu.make_async_remote_copy(
@@ -694,14 +727,17 @@
         total = total + r.second[c]
     r.third[seq] = total
     run(NSEQ, make_d)()
+    lax.fori_loop(0, CH // 2, sent, 0)
+    for i in range(4):
+        relay(i).wait_send()
     for copy in results:
         copy.wait()
 
 
 def write_kernel(
     i_val, i_gin, i_gout, i_second, i_third, skip,
-    o_val, o_gin, o_gout, g_skip, g_in, g_bin, g_mid, g_bmid, g_out, g_rate,
-    stage, second, third, in_sem, out_sem, small_sem,
+    o_val, o_gin, o_gout, o_skip, o_in, o_bin, o_mid, o_bmid, o_out, o_rate,
+    stage, second, third, g_skip, g_in, g_bin, g_mid, g_bmid, g_out, g_rate, in_sem, out_sem, small_sem,
 ):
     loads, stores = [], []
     for i, (src, dst) in enumerate(((i_val, o_val), (i_gin, o_gin), (i_gout, o_gout))):
@@ -711,10 +747,10 @@
     small = [
         pltpu.make_async_copy(i_second, second, small_sem.at[0]),
         pltpu.make_async_copy(i_third, third, small_sem.at[1]),
+        pltpu.make_async_copy(skip, g_skip, small_sem.at[2]),
     ]
     for copy in small + loads:
         copy.start()
-    g_skip[...] = skip[...]
     for load, store in zip(loads, stores):
         load.wait()
         store.start()
@@ -730,6 +766,14 @@
     own = jnp.transpose(second[...].reshape(128, 256)[:, 128:256])
     g_out[...] = own[48:112, :]
     g_rate[...] = own[112:113, :]
+    pairs = (
+        (g_skip, o_skip), (g_in, o_in), (g_bin, o_bin), (g_mid, o_mid), (g_bmid, o_bmid), (g_out, o_out),
+        (g_rate, o_rate),
+    )
+    for i, (src, dst) in enumerate(pairs):
+        copy = pltpu.make_async_copy(src, dst, small_sem.at[3 + i])
+        copy.start()
+        stores.append(copy)
     for copy in stores:
         copy.wait()
 
@@ -768,7 +812,8 @@
         out_specs=[HB] * 3 + [VM] * 3,
         scratch_shapes=[pltpu.VMEM(shape, dtype) for shape, dtype in SCRATCH.values()]
         + [
-            DMA((N_LOCAL,)), DMA((6,)), DMA((9,)), DMA((9,)), DMA((9,)), DMA((9,)),
+            DMA((N_LOCAL,)), DMA((6,)), DMA((5, 4)), DMA((5, 4)), DMA((4,)), DMA((4,)),
+            DMA((4, 4)), DMA((4, 4)), DMA((4, 5)), DMA((4, 5)), DMA((NSEQ,)), DMA((NSEQ,)),
             DMA((NSEQ,)), DMA((NSEQ,)), DMA((NCHAN,)), DMA((NCHAN,)), DMA((NSEQ,)), DMA((NSEQ,)),
         ],
         compiler_params=pltpu.CompilerParams(
@@ -782,11 +827,14 @@
             big, big, big, sds((1, CH)), sds((33, 64)), sds((1, 64)), sds((2, 64, 64)), sds((2, 64)),
             sds((64, 128)), sds((1, 128)),
         ],
-        in_specs=[HB] * 5 + [VM],
-        out_specs=[HB] * 3 + [VM] * 7,
+        in_specs=[HB] * 6,
+        out_specs=[HB] * 10,
         scratch_shapes=[
             pltpu.VMEM((3,) + BIG, LOW), pltpu.VMEM((NCHAN, 8, 256), F32), pltpu.VMEM((NSEQ, 8, 256), F32),
-            DMA((6,)), DMA((6,)), DMA((2,)),
+            pltpu.VMEM((1, CH), F32), pltpu.VMEM((33, 64), F32), pltpu.VMEM((1, 64), F32),
+            pltpu.VMEM((2, 64, 64), F32), pltpu.VMEM((2, 64), F32), pltpu.VMEM((64, 128), F32),
+            pltpu.VMEM((1, 128), F32),
+            DMA((6,)), DMA((6,)), DMA((10,)),
         ],
         compiler_params=pltpu.CompilerParams(vmem_limit_bytes=VMEM_MAIN),
         name="write_results",

time: 64.4 us -> 60.4 us (0.938)
  Pallas kernels: 63.6 us -> 59.6 us
    pallas_call x1, Pallas kernels: 59.5 us -> 56.6 us  [local(): pl.pallas_call(main_kernel, out_shape=[big, big, big, sds((NCHAN, 8, 256)...]
    pallas_call x1, Pallas kernels: 4.08 us -> 2.93 us  [local(): pl.pallas_call(write_kernel, out_shape=[big, big, big, sds((1, CH)), sds(...]
where the time goes in v2:
time: 60.4 us; the launch traced here: 60.2 us
  Pallas kernels  59.6 us (99%)
  between operations  0.66 us (1%)
    pallas_call x1, Pallas kernels, local(): pl.pallas_call(main_kernel, out_shape=[big, big, big, sds((NCHAN, 8, 256)...  56.6 us
    pallas_call x1, Pallas kernels, local(): pl.pallas_call(write_kernel, out_shape=[big, big, big, sds((1, CH)), sds(...  2.93 us

profile of v2, /device:TPU:1, one launch (start us, length us, event | category | flops | bytes accessed | tf_op | source)
XLA Modules:
  0.0 60.2 jit_solution(256210836620658264)
XLA Ops:
  0.6 56.6 %hyena_backward.1 = (bf16[2,256,8,128]{3,2,1,0:T(8,128)(2,1)}, bf16[2,256,8,128]{3,2,1,0:T(8,128)(2,1)}, bf16[2,256,8,128]{3,2,1,0:T(8,128)(2,1)}, f32[16,8,256]...) custom-call(s32[2,48,128]{2,1,0:T(8,128)} %constant.12.clone.refs_0_, f32[33,64]{1,0:T(8,128)} %bitcast.36, ...), custom_call_target="tpu_custom_call" | custom-call | tf_op jit(solution)/shard_map/hyena_backward/pallas_call | solution.py:808
  57.3 2.9 %write_results.1 = (bf16[2,256,8,128]{3,2,1,0:T(8,128)(2,1)}, bf16[2,256,8,128]{3,2,1,0:T(8,128)(2,1)}, bf16[2,256,8,128]{3,2,1,0:T(8,128)(2,1)}, f32[1,8]{1,0:T...) custom-call(bf16[2,256,8,128]{3,2,1,0:T(8,128)(2,1)} %get-tuple-elem, ...), custom_call_target="tpu_custom_call" | custom-call | tf_op jit(solution)/shard_map/write_results/pallas_call | solution.py:824

commit v3 on v2

--- a/solution.py
+++ b/solution.py
@@ -65,8 +65,8 @@
 def poly_fit():
     x = (np.cos(np.pi * (np.arange(64) + 0.5) / 64) + 1) / 2 * (np.pi / 2 * 1.002) ** 2
     r = np.sqrt(x)
-    sin_c = np.polynomial.polynomial.polyfit(x, np.sin(r) / r, 5)
-    cos_c = np.polynomial.polynomial.polyfit(x, np.cos(r), 6)
+    sin_c = np.polynomial.polynomial.polyfit(x, np.sin(r) / r, 4)
+    cos_c = np.polynomial.polynomial.polyfit(x, np.cos(r), 5)
     return [float(v) for v in sin_c], [float(v) for v in cos_c]
 
 
@@ -355,16 +355,18 @@
         r.gk[2 * p + i] = ys[i]
 
 
+def channel_stats(r, c):
+    x = r.raw_flat[channel_rows(c), :]
+    r.stat[0, pl.ds(c, 1), :] = jnp.sum(x * x, axis=0, keepdims=True)
+    r.stat[1, pl.ds(c, 1), :] = jnp.sum(x * r.gk[c], axis=0, keepdims=True)
+
+
 def filter_products(r, p):
     kernels = []
     for i in range(2):
         c = 2 * p + i
-        x = r.raw_flat[channel_rows(c), :]
-        square = jnp.sum(x * x, axis=0, keepdims=True)
-        r.stat[0, pl.ds(c, 1), :] = square
-        r.stat[1, pl.ds(c, 1), :] = jnp.sum(x * r.gk[c], axis=0, keepdims=True)
-        norm = jnp.sqrt(jnp.sum(square, axis=1, keepdims=True) + EPSILON)
-        kernels.append(to_low(x / norm))
+        square = jnp.sum(r.stat[0, pl.ds(c, 1), :], axis=1, keepdims=True)
+        kernels.append(to_low(r.raw_flat[channel_rows(c), :] * (1.0 / jnp.sqrt(square + EPSILON))))
     fk = forward_pair(r, jnp.concatenate(kernels, axis=1))
     for i in range(2):
         c = 2 * p + i
@@ -406,7 +408,7 @@
 SMALL = ("bands", "w_in", "b_in", "w_mid", "b_mid", "w_out", "rate", "skip")
 TABLES = ("w1", "w1t", "fwd", "inv", "turn")
 LARGE = ("val", "gin", "cot", "gout")
-OUTS = ("h_val", "h_gin", "h_gout", "second", "third", "g_skip")
+OUTS = ("h_val", "h_gin", "h_gout", "own", "third", "g_skip")
 BIG = (2, A, CH, B)
 FULL = (2, A * CH, B)
 SCRATCH = {
@@ -463,6 +465,7 @@
     "block": ((2, 64, 128), F32),
     "share": ((NSEQ, 8, 256), F32),
     "first": ((NSEQ, 8, 256), F32),
+    "second": ((16, 8, 256), F32),
 }
 N_LOCAL = len(SMALL) + len(TABLES) + len(LARGE)
 
@@ -482,12 +485,28 @@
     def signal(device):
         pl.semaphore_signal(barrier, inc=1, device_id=device, device_id_type=MESH)
 
-    def hail_seq(d, carry):
-        signal((chan, lax.rem(seq + d, NSEQ)))
-        return carry
-
-    def hail_chan(d, carry):
-        signal((lax.rem(chan + d, NCHAN), seq))
+    x, z = lax.div(seq, 2), lax.rem(seq, 2)
+    yz, core = lax.div(chan, 2), lax.rem(chan, 2)
+    first_id, second_id = 2 * x + core, 2 * yz + z
+
+    def seq_peer(d):
+        return (chan, lax.rem(seq + d, NSEQ))
+
+    def first_peer(d):
+        to = lax.rem(first_id + d, 8)
+        return (2 * yz + lax.rem(to, 2), 2 * lax.div(to, 2) + z)
+
+    def second_peer(d):
+        to = lax.rem(second_id + d, 16)
+        return (2 * lax.div(to, 2) + core, 2 * x + lax.rem(to, 2))
+
+    def hail(d, carry):
+        signal(seq_peer(d))
+        signal(first_peer(d))
+        return carry
+
+    def hail_second(d, carry):
+        signal(second_peer(d))
         return carry
 
     loads = {}
@@ -495,14 +514,13 @@
         loads[name] = pltpu.make_async_copy(ins[i], getattr(r, name), load_sem.at[i])
     for name in SMALL:
         loads[name].start()
-    lax.fori_loop(1, NSEQ, hail_seq, 0)
-    lax.fori_loop(1, NCHAN, hail_chan, 0)
+    lax.fori_loop(1, 8, hail, 0)
+    lax.fori_loop(1, 16, hail_second, 0)
     for name in LARGE + TABLES:
         loads[name].start()
     for name in SMALL:
         loads[name].wait()
 
-    x, z = lax.div(seq, 2), lax.rem(seq, 2)
     xr, xl, xo = lax.rem(x + 1, 4), lax.rem(x + 3, 4), lax.rem(x + 2, 4)
     other = 1 - z
     near = (
@@ -583,7 +601,7 @@
             near_block(p, i).start()
 
     prepare_weights(r, chan)
-    pl.semaphore_wait(barrier, NSEQ - 1 + NCHAN - 1)
+    pl.semaphore_wait(barrier, 7 + 7 + 15)
     net_forward(r, seq, send_chunk)
 
     for name in LARGE:
@@ -603,13 +621,16 @@
         arrived(3 + i, n_piece // 2, n_piece)
         relay(2 + i).start()
 
+    spectra(r, 1)
+    scatter_far(1)
+
     def pair_step(p, carry):
         spectra(r, p)
         scatter_far(p)
-        scatter_near(p - 1)
-        return carry
-
-    lax.fori_loop(1, CH // 2, pair_step, 0)
+        scatter_near(p - 2)
+        return carry
+
+    lax.fori_loop(2, CH // 2, pair_step, 0)
     arrived(0, 0, n_piece)
     for i in range(2):
         arrived(1 + i, n_piece // 2, n_piece)
@@ -617,14 +638,11 @@
     for i in range(4):
         relay(i).wait_recv()
 
-    filter_products(r, 0)
-    scatter_near(CH // 2 - 1)
-
-    def product_step(p, carry):
-        filter_products(r, p)
-        return carry
-
-    lax.fori_loop(1, CH // 2, product_step, 0)
+    def stats_step(c, carry):
+        channel_stats(r, c)
+        return carry
+
+    lax.fori_loop(0, CH, stats_step, 0)
 
     def run(size, make):
         def start(d, carry):
@@ -637,9 +655,6 @@
 
         lax.fori_loop(1, size, start, 0)
         return lambda: lax.fori_loop(1, size, wait, 0)
-
-    def seq_peer(d):
-        return (chan, lax.rem(seq + d, NSEQ))
 
     def make_a(d):
         return pltpu.make_async_remote_copy(
@@ -648,6 +663,19 @@
         )
 
     wait_along = run(NSEQ, make_a)
+
+    def product_step(p, carry):
+        filter_products(r, p)
+        scatter_near(p + CH // 2 - 2)
+        return carry
+
+    lax.fori_loop(0, 2, product_step, 0)
+
+    def last_step(p, carry):
+        filter_products(r, p)
+        return carry
+
+    lax.fori_loop(2, CH // 2, last_step, 0)
     results = []
 
     def leave(n):
@@ -694,39 +722,51 @@
 
     def make_b(d):
         return pltpu.make_async_remote_copy(
-            src_ref=r.share.at[lax.rem(seq + d, NSEQ)], dst_ref=r.first.at[d],
-            send_sem=sem_b.at[d], recv_sem=recv_b.at[d], device_id=seq_peer(d), device_id_type=MESH,
+            src_ref=r.share.at[lax.rem(first_id + d, 8)], dst_ref=r.first.at[d],
+            send_sem=sem_b.at[d], recv_sem=recv_b.at[d], device_id=first_peer(d), device_id_type=MESH,
         )
 
     def make_c(d):
         return pltpu.make_async_remote_copy(
-            src_ref=r.second.at[chan], dst_ref=r.second.at[chan], send_sem=sem_c.at[d], recv_sem=recv_c.at[d],
-            device_id=(lax.rem(chan + d, NCHAN), seq), device_id_type=MESH,
+            src_ref=r.second.at[second_id], dst_ref=r.second.at[second_id],
+            send_sem=sem_c.at[d], recv_sem=recv_c.at[d], device_id=second_peer(d), device_id_type=MESH,
         )
 
     def make_d(d):
         return pltpu.make_async_remote_copy(
-            src_ref=r.third.at[seq], dst_ref=r.third.at[seq], send_sem=sem_d.at[d], recv_sem=recv_d.at[d],
-            device_id=seq_peer(d), device_id_type=MESH,
+            src_ref=r.third.at[first_id], dst_ref=r.third.at[first_id],
+            send_sem=sem_d.at[d], recv_sem=recv_d.at[d], device_id=first_peer(d), device_id_type=MESH,
         )
 
-    wait = run(NSEQ, make_b)
+    wait = run(8, make_b)
     finish(r, 1)
     leave(1)
     wait()
-    total = r.share[seq]
-    for d in range(1, NSEQ):
-        total = total + r.first[d]
+    same = r.share[first_id]
+    for d in range(2, 8, 2):
+        same = same + r.first[d]
+    both = same
+    for d in range(1, 8, 2):
+        both = both + r.first[d]
     factor = 1.0 / math.sqrt(16 * L)
-    total = total * factor
-    r.second[chan] = total
-    r.g_skip[...] = to_row(total[:, 241:242])
-    run(NCHAN, make_c)()
+    r.second[second_id] = jnp.where(iota((8, 256), 1) < 176, both, same) * factor
+    run(16, make_c)()
     total = r.second[0]
-    for c in range(1, NCHAN):
+    for c in range(1, 16):
         total = total + r.second[c]
-    r.third[seq] = total
-    run(NSEQ, make_d)()
+    r.third[first_id] = total
+    for c in range(8):
+        r.own[c, core] = r.second[2 * c, :, 128:256] + r.second[2 * c + 1, :, 128:256]
+    wait = run(8, make_d)
+    part = r.own.at[:, core]
+    swap = pltpu.make_async_remote_copy(
+        src_ref=part, dst_ref=part, send_sem=sem_d.at[0], recv_sem=recv_d.at[0],
+        device_id=(2 * yz + 1 - core, seq), device_id_type=MESH,
+    )
+    swap.start()
+    r.g_skip[...] = to_row(r.own[yz, core][:, 113:114])
+    wait()
+    swap.wait()
     lax.fori_loop(0, CH // 2, sent, 0)
     for i in range(4):
         relay(i).wait_send()
@@ -763,7 +803,7 @@
     g_in[...] = flat[0:33, :]
     g_bin[...] = flat[33:34, :]
     g_bmid[...] = flat[34:36, :]
-    own = jnp.transpose(second[...].reshape(128, 256)[:, 128:256])
+    own = jnp.transpose(second[...].reshape(128, 128))
     g_out[...] = own[48:112, :]
     g_rate[...] = own[112:113, :]
     pairs = (
@@ -805,9 +845,9 @@
     )
     large = tuple(to_natural(x) for x in (value, gate_in, cotangent, gate_out))
     big = sds(BIG, LOW)
-    o_val, o_gin, o_gout, second, third, g_skip = pl.pallas_call(
+    o_val, o_gin, o_gout, own, third, g_skip = pl.pallas_call(
         main_kernel,
-        out_shape=[big, big, big, sds((NCHAN, 8, 256)), sds((NSEQ, 8, 256)), sds((1, CH))],
+        out_shape=[big, big, big, sds((8, 2, 8, 128)), sds((NSEQ, 8, 256)), sds((1, CH))],
         in_specs=[HB] * N_LOCAL,
         out_specs=[HB] * 3 + [VM] * 3,
         scratch_shapes=[pltpu.VMEM(shape, dtype) for shape, dtype in SCRATCH.values()]
@@ -830,7 +870,7 @@
         in_specs=[HB] * 6,
         out_specs=[HB] * 10,
         scratch_shapes=[
-            pltpu.VMEM((3,) + BIG, LOW), pltpu.VMEM((NCHAN, 8, 256), F32), pltpu.VMEM((NSEQ, 8, 256), F32),
+            pltpu.VMEM((3,) + BIG, LOW), pltpu.VMEM((8, 2, 8, 128), F32), pltpu.VMEM((NSEQ, 8, 256), F32),
             pltpu.VMEM((1, CH), F32), pltpu.VMEM((33, 64), F32), pltpu.VMEM((1, 64), F32),
             pltpu.VMEM((2, 64, 64), F32), pltpu.VMEM((2, 64), F32), pltpu.VMEM((64, 128), F32),
             pltpu.VMEM((1, 128), F32),
@@ -838,7 +878,7 @@
         ],
         compiler_params=pltpu.CompilerParams(vmem_limit_bytes=VMEM_MAIN),
         name="write_results",
-    )(o_val, o_gin, o_gout, second, third, g_skip)
+    )(o_val, o_gin, o_gout, own, third, g_skip)
     return (
         from_natural(o_val), from_natural(o_gin), from_natural(o_gout), g_skip.reshape(CH),
         g_in.T, g_bin.reshape(64), g_mid, g_bmid, g_out.T, g_rate.reshape(128),

time: 60.4 us -> 55.2 us (0.914)
  Pallas kernels: 59.6 us -> 54.4 us
    pallas_call x1, Pallas kernels: 56.6 us -> 51.5 us  [local(): pl.pallas_call(main_kernel, out_shape=[big, big, big, sds((8, 2, 8, 128))...]
where the time goes in v3:
time: 55.2 us; the launch traced here: 55.1 us
  Pallas kernels  54.4 us (99%)
  between operations  0.66 us (1%)
    pallas_call x1, Pallas kernels, local(): pl.pallas_call(main_kernel, out_shape=[big, big, big, sds((8, 2, 8, 128))...  51.5 us
    pallas_call x1, Pallas kernels, local(): pl.pallas_call(write_kernel, out_shape=[big, big, big, sds((1, CH)), sds(...  2.93 us

profile of v3, /device:TPU:1, one launch (start us, length us, event | category | flops | bytes accessed | tf_op | source)
XLA Modules:
  0.0 55.1 jit_solution(484839381144499489)
XLA Ops:
  0.6 51.5 %hyena_backward.1 = (bf16[2,256,8,128]{3,2,1,0:T(8,128)(2,1)}, bf16[2,256,8,128]{3,2,1,0:T(8,128)(2,1)}, bf16[2,256,8,128]{3,2,1,0:T(8,128)(2,1)}, f32[8,2,8,128...) custom-call(s32[2,48,128]{2,1,0:T(8,128)} %constant.12.clone.refs_0_, f32[33,64]{1,0:T(8,128)} %bitcast.36, ...), custom_call_target="tpu_custom_call" | custom-call | tf_op jit(solution)/shard_map/hyena_backward/pallas_call | solution.py:848
  52.1 2.9 %write_results.1 = (bf16[2,256,8,128]{3,2,1,0:T(8,128)(2,1)}, bf16[2,256,8,128]{3,2,1,0:T(8,128)(2,1)}, bf16[2,256,8,128]{3,2,1,0:T(8,128)(2,1)}, f32[1,8]{1,0:T...) custom-call(bf16[2,256,8,128]{3,2,1,0:T(8,128)(2,1)} %get-tuple-elem, ...), custom_call_target="tpu_custom_call" | custom-call | tf_op jit(solution)/shard_map/write_results/pallas_call | solution.py:864

commit v4 on v3

--- a/solution.py
+++ b/solution.py
@@ -152,7 +152,7 @@
         self.__dict__.update(refs)
 
 
-def prepare_weights(r, chan):
+def prepare_weights(r, chan, other):
     first = jnp.where(iota((8, 64), 0) == 1, jnp.broadcast_to(r.b_in[...], (8, 64)), 0.0)
     r.w_pad[0:32, :] = r.w_in[0:32, :]
     r.w_pad[32:40, :] = jnp.where(iota((8, 64), 0) == 0, jnp.broadcast_to(r.w_in[32:33, :], (8, 64)), first)
@@ -163,11 +163,14 @@
         w = r.w_mid[i]
         r.k_mid[i] = hi_hi_lo(dot_full(w, rep), 64)
         r.k_back[i] = hi_hi_lo(dot_tn(w, rep, HIGHEST), 64)
-    own = jnp.where(iota((CH, 128), 1) == iota((CH, 128), 0) + chan * CH, 1.0, 0.0)
-    w_own = dot_nt(own, r.w_out[...], HIGHEST)
+    row = iota((2 * CH, 128), 0)
+    channel = jnp.where(row < CH, row + chan * CH, row - CH + other * CH)
+    pick = jnp.where(iota((2 * CH, 128), 1) == channel, 1.0, 0.0)
+    w_own = dot_nt(pick, r.w_out[...], HIGHEST)
     r.k_out[...] = hi_hi_lo(dot_full(w_own, rep), 64)
-    r.k_outback[...] = hi_hi_lo(dot_tn(w_own, repeat_matrix(CH, CH, 4), HIGHEST), CH)
-    r.rate_col[...] = jnp.broadcast_to(to_column(r.rate[...], CH, chan * CH), (CH, 128))
+    r.k_outback[...] = hi_hi_lo(dot_tn(w_own, repeat_matrix(2 * CH, 2 * CH, 3), HIGHEST), 2 * CH)
+    rates = jnp.sum(jnp.where(pick > 0.5, jnp.broadcast_to(r.rate[...], (2 * CH, 128)), 0.0), axis=1, keepdims=True)
+    r.rate_col[...] = jnp.broadcast_to(rates, (2 * CH, 128))
     r.bias_col[0] = jnp.broadcast_to(to_column(r.b_mid[0:1, :], 64, 0), (64, 128))
     r.bias_col[1] = jnp.broadcast_to(to_column(r.b_mid[1:2, :], 64, 0), (64, 128))
 
@@ -176,18 +179,18 @@
     return jnp.concatenate([block] * times, axis=1)
 
 
-def fraction(seq, base):
-    pos = seq * TB + base + iota((CH, CHUNK), 1)
+def fraction(base):
+    pos = base + iota((2 * CH, CHUNK), 1)
     return pos.astype(F32) * (1.0 / L)
 
 
-def net_forward(r, seq, send):
+def net_forward(r, seq, core, send):
     per = CHUNK // 128
 
     def step(j, carry):
         base = pl.multiple_of(j * CHUNK, CHUNK)
         lanes = pl.ds(base, CHUNK)
-        pos = seq * TB + base + iota((48, CHUNK), 1)
+        pos = seq * TB + (2 * core + j) * CHUNK + iota((48, CHUNK), 1)
         row = iota((48, CHUNK), 0)
         phase = ((wide(r.bands[0], per) * pos + (wide(r.bands[1], per) + L // 2)) & (L - 1)) - L // 2
         phase = jnp.where(phase > L // 4, L // 2 - phase, phase)
@@ -209,16 +212,17 @@
             x = jnp.concatenate([hi, lo, hi], axis=0)
             if layer < 2:
                 z = low_dot(r.k_mid[layer], x) + wide(r.bias_col[layer], per)
-        raw = low_dot(r.k_out[...], x) * jnp.exp(-wide(r.rate_col[...], per) * frac[0:CH, :])
+        raw = low_dot(r.k_out[...], x) * jnp.exp(-wide(r.rate_col[...], per) * frac[0 : 2 * CH, :])
         for i in range(per):
-            r.raw_all[seq * ABLK + j * per + i] = raw[:, 128 * i : 128 * i + 128]
+            r.raw_all[seq * ABLK + (2 * core + j) * per + i] = raw[0:CH, 128 * i : 128 * i + 128]
+            r.raw_other[j * per + i] = raw[CH:, 128 * i : 128 * i + 128]
         send(j)
         return carry
 
-    lax.fori_loop(0, TB // CHUNK, step, 0)
-
-
-def net_backward(r, seq, scale_gk, scale_raw):
+    lax.fori_loop(0, TB // CHUNK // 2, step, 0)
+
+
+def net_backward(r, seq, core):
     per = CHUNK // 128
     r.acc[...] = jnp.zeros_like(r.acc)
     r.acc_out[...] = jnp.zeros_like(r.acc_out)
@@ -233,18 +237,23 @@
 
     def step(j, carry):
         lanes = pl.ds(pl.multiple_of(j * CHUNK, CHUNK), CHUNK)
-        start = seq * ABLK + j * per
-        grad = jnp.concatenate([r.total[pl.ds(j * per + i, CH, stride=ABLK), :] for i in range(per)], axis=1)
-        raw = jnp.concatenate([r.raw_all[start + i] for i in range(per)], axis=1)
-        grad = grad * wide(scale_gk, per) - raw * wide(scale_raw, per)
-        frac = fraction(seq, j * CHUNK)
+        start = (2 * core + j) * per
+
+        def rows(mine, first, others, second):
+            return jnp.concatenate(
+                [jnp.concatenate([mine[first + i], others[second + i]], axis=0) for i in range(per)], axis=1
+            )
+
+        grad = rows(r.grad_own, start, r.grad_other, j * per)
+        raw = rows(r.raw_all, seq * ABLK + start, r.raw_other, j * per)
+        frac = fraction(seq * TB + (2 * core + j) * CHUNK)
         r.acc_rate[...] -= lane_sum(grad * raw * frac)
         shaped = grad * jnp.exp(-wide(r.rate_col[...], per) * frac)
         hi = shaped.astype(LOW).astype(F32)
         lo = shaped - hi
         pair = jnp.concatenate([hi, lo], axis=0).astype(LOW)
         r.acc_out[...] += dot_nt(pair, r.act[2, :, lanes])
-        d = low_dot(r.k_outback[...], jnp.concatenate([hi, lo, hi, jnp.zeros_like(hi)], axis=0).astype(LOW))
+        d = low_dot(r.k_outback[...], jnp.concatenate([hi, lo, hi], axis=0).astype(LOW))
         for layer in (2, 1, 0):
             d = d * r.der[layer, :, lanes]
             hi, lo = split(d)
@@ -257,7 +266,7 @@
                 r.acc[0] += dot_nt(pair, r.feat[:, lanes])
         return carry
 
-    lax.fori_loop(0, TB // CHUNK, step, 0)
+    lax.fori_loop(0, TB // CHUNK // 2, step, 0)
 
 
 def fold_halves(x):
@@ -266,21 +275,25 @@
     return total + pltpu.roll(total, 64, 1)
 
 
-def pack_shares(r):
+def pack_shares(r, core):
     lane = iota((64, 128), 1)
     r.block[0] = jnp.where(lane < 64, fold_halves(r.acc[1]), fold_halves(r.acc[2]))
     block = fold_halves(r.acc[0])
     block = jnp.where(lane == 34, jnp.sum(r.acc_bias[0], axis=1, keepdims=True), block)
     r.block[1] = jnp.where(lane == 35, jnp.sum(r.acc_bias[1], axis=1, keepdims=True), block)
-    lane = iota((CH, 128), 1)
+    lane = iota((2 * CH, 128), 1)
     own = pltpu.roll(fold_halves(r.acc_out[...]), 48, 1)
     own = jnp.where(lane == 112, jnp.sum(r.acc_rate[...], axis=1, keepdims=True), own)
-    own = jnp.where(lane == 113, r.skip_part[...], own)
+    own = jnp.where(lane > 112, 0.0, own)
+    lane = iota((CH, 128), 1)
+    theirs = own[CH:]
+    own = jnp.where(lane == 113, r.skip_part[...], own[0:CH])
 
     def place(s, carry):
         rows = pl.ds(pl.multiple_of(8 * s, 8), 8)
         r.share[s, :, 0:128] = r.block[0, rows, :]
-        r.share[s, :, 128:256] = jnp.where(lane < 48, r.block[1, rows, :], own)
+        apart = jnp.where(lax.rem(s, 2) == core, own, theirs)
+        r.share[s, :, 128:256] = jnp.where(lane < 48, r.block[1, rows, :], apart)
         return carry
 
     lax.fori_loop(0, NSEQ, place, 0)
@@ -436,14 +449,17 @@
     "k_in": ((64, 144), LOW),
     "k_mid": ((2, 64, 192), LOW),
     "k_back": ((2, 64, 192), LOW),
-    "k_out": ((CH, 192), LOW),
-    "k_outback": ((64, 4 * CH), LOW),
-    "rate_col": ((CH, 128), F32),
+    "k_out": ((2 * CH, 192), LOW),
+    "k_outback": ((64, 6 * CH), LOW),
+    "rate_col": ((2 * CH, 128), F32),
     "bias_col": ((2, 64, 128), F32),
-    "feat": ((128, TB), LOW),
-    "act": ((3, 128, TB), LOW),
-    "der": ((3, 64, TB), F32),
+    "feat": ((128, TB // 2), LOW),
+    "act": ((3, 128, TB // 2), LOW),
+    "der": ((3, 64, TB // 2), F32),
     "raw_all": ((A, CH, B), F32),
+    "raw_other": ((ABLK // 2, CH, B), F32),
+    "grad_own": ((ABLK, CH, B), F32),
+    "grad_other": ((ABLK // 2, CH, B), F32),
     "total": ((CH * ABLK, B), F32),
     "half": ((CH // 2, 2, 2, 2, ABLK // 2, B), F32),
     "side_out": ((CH // 2, 2, 2, 2, ABLK, B), F32),
@@ -458,9 +474,9 @@
     "conv": (FULL, F32),
     "back": (FULL, F32),
     "acc": ((3, 128, 128), F32),
-    "acc_out": ((16, 128), F32),
+    "acc_out": ((4 * CH, 128), F32),
     "acc_bias": ((2, 64, 128), F32),
-    "acc_rate": ((CH, 128), F32),
+    "acc_rate": ((2 * CH, 128), F32),
     "skip_part": ((CH, 1), F32),
     "block": ((2, 64, 128), F32),
     "share": ((NSEQ, 8, 256), F32),
@@ -476,7 +492,7 @@
     names = list(SCRATCH)
     scratch = refs[N_LOCAL + len(OUTS) :]
     r = Refs(**dict(zip(OUTS, outs)), **dict(zip(names, scratch)))
-    (load_sem, out_sem, ag_send, ag_recv, relay_send, relay_recv, half_send, half_recv, rs_send, rs_recv,
+    (load_sem, out_sem, ag_send, ag_recv, cross_send, relay_send, relay_recv, half_send, half_recv, rs_send, rs_recv,
      sem_a, recv_a, sem_b, recv_b, sem_c, recv_c, sem_d, recv_d) = scratch[len(names) :]
     r.raw_flat = r.raw_all.reshape(A * CH, B)
     chan, seq = lax.axis_index("chan"), lax.axis_index("seq")
@@ -488,6 +504,13 @@
     x, z = lax.div(seq, 2), lax.rem(seq, 2)
     yz, core = lax.div(chan, 2), lax.rem(chan, 2)
     first_id, second_id = 2 * x + core, 2 * yz + z
+
+    xr, xl, xo = lax.rem(x + 1, 4), lax.rem(x + 3, 4), lax.rem(x + 2, 4)
+    other = 1 - z
+    near_seq = (2 * x + other, 2 * xr + z, 2 * xr + other, 2 * xl + z, 2 * xl + other)
+    near = tuple((chan, to) for to in near_seq)
+    across = tuple((2 * yz + 1 - core, to) for to in near_seq + (seq,))
+    to_r, to_l = near[1], near[3]
 
     def seq_peer(d):
         return (chan, lax.rem(seq + d, NSEQ))
@@ -516,17 +539,13 @@
         loads[name].start()
     lax.fori_loop(1, 8, hail, 0)
     lax.fori_loop(1, 16, hail_second, 0)
+    for i in range(5):
+        signal(across[i])
     for name in LARGE + TABLES:
         loads[name].start()
     for name in SMALL:
         loads[name].wait()
 
-    xr, xl, xo = lax.rem(x + 1, 4), lax.rem(x + 3, 4), lax.rem(x + 2, 4)
-    other = 1 - z
-    near = (
-        (chan, 2 * x + other), (chan, 2 * xr + z), (chan, 2 * xr + other), (chan, 2 * xl + z), (chan, 2 * xl + other)
-    )
-    to_r, to_l = near[1], near[3]
     half = ABLK // 2
     piece = CHUNK // 128
     n_piece = ABLK // piece
@@ -541,9 +560,19 @@
             device_id=near[i], device_id_type=MESH,
         )
 
+    def cross(i, j):
+        return pltpu.make_async_remote_copy(
+            src_ref=r.raw_other.at[pl.ds(j * piece, piece)],
+            dst_ref=r.raw_all.at[pl.ds(row_of(x, z) + (2 * core + j) * piece, piece)],
+            send_sem=cross_send.at[i, j], recv_sem=ag_recv.at[i, 2 * core + j],
+            device_id=across[i], device_id_type=MESH,
+        )
+
     def send_chunk(j):
         for i in range(5):
-            gather(i, j).start()
+            gather(i, 2 * core + j).start()
+        for i in range(6):
+            cross(i, j).start()
 
     def relay(i):
         row = row_of(xl if i < 2 else xr, (z, other)[i % 2]) + (0 if i < 2 else half)
@@ -551,6 +580,13 @@
         return pltpu.make_async_remote_copy(
             src_ref=part, dst_ref=part, send_sem=relay_send.at[i], recv_sem=relay_recv.at[i],
             device_id=to_r if i < 2 else to_l, device_id_type=MESH,
+        )
+
+    def own_half(j):
+        part = r.raw_all.at[pl.ds(row_of(x, z) + (2 * (1 - core) + j) * piece, piece)]
+        return pltpu.make_async_remote_copy(
+            src_ref=part, dst_ref=part, send_sem=cross_send.at[5, j], recv_sem=ag_recv.at[5, 2 * (1 - core) + j],
+            device_id=across[5], device_id_type=MESH,
         )
 
     def arrived(i, start, stop):
@@ -600,9 +636,9 @@
         for i in range(1, 5):
             near_block(p, i).start()
 
-    prepare_weights(r, chan)
-    pl.semaphore_wait(barrier, 7 + 7 + 15)
-    net_forward(r, seq, send_chunk)
+    prepare_weights(r, chan, 2 * yz + 1 - core)
+    pl.semaphore_wait(barrier, 7 + 7 + 15 + 5)
+    net_forward(r, seq, core, send_chunk)
 
     for name in LARGE:
         loads[name].wait()
@@ -632,6 +668,8 @@
 
     lax.fori_loop(2, CH // 2, pair_step, 0)
     arrived(0, 0, n_piece)
+    for j in range(2):
+        own_half(j).wait_recv()
     for i in range(2):
         arrived(1 + i, n_piece // 2, n_piece)
         arrived(3 + i, 0, n_piece // 2)
@@ -709,16 +747,40 @@
     scale_gk = jnp.broadcast_to((1.0 / L) / norm, (CH, B))
     scale_raw = jnp.broadcast_to(along / (norm * norm * norm), (CH, B))
 
+    def gradient(half_id):
+        def step(i, carry):
+            row = half_id * half + i
+            total = r.total[pl.ds(row, CH, stride=ABLK), :]
+            r.grad_own[row] = total * scale_gk - r.raw_all[row_of(x, z) + row] * scale_raw
+            return carry
+
+        lax.fori_loop(0, half, step, 0, unroll=4)
+
+    gradient(1 - core)
+    hand = pltpu.make_async_remote_copy(
+        src_ref=r.grad_own.at[pl.ds((1 - core) * half, half)], dst_ref=r.grad_other,
+        send_sem=sem_a.at[0], recv_sem=recv_a.at[0], device_id=across[5], device_id_type=MESH,
+    )
+    hand.start()
+    gradient(core)
+    hand.wait()
+
     def sent(j, carry):
         for i in range(5):
-            gather(i, j).wait_send()
             near_block(j, i).wait_send()
         for i in range(4):
             far_half(j, i // 2, i % 2).wait_send()
         return carry
 
-    net_backward(r, seq, scale_gk, scale_raw)
-    pack_shares(r)
+    def sent_raw(j, carry):
+        for i in range(5):
+            gather(i, 2 * core + j).wait_send()
+        for i in range(6):
+            cross(i, j).wait_send()
+        return carry
+
+    net_backward(r, seq, core)
+    pack_shares(r, core)
 
     def make_b(d):
         return pltpu.make_async_remote_copy(
@@ -742,14 +804,11 @@
     finish(r, 1)
     leave(1)
     wait()
-    same = r.share[first_id]
-    for d in range(2, 8, 2):
-        same = same + r.first[d]
-    both = same
-    for d in range(1, 8, 2):
+    both = r.share[first_id]
+    for d in range(1, 8):
         both = both + r.first[d]
     factor = 1.0 / math.sqrt(16 * L)
-    r.second[second_id] = jnp.where(iota((8, 256), 1) < 176, both, same) * factor
+    r.second[second_id] = both * factor
     run(16, make_c)()
     total = r.second[0]
     for c in range(1, 16):
@@ -768,6 +827,7 @@
     wait()
     swap.wait()
     lax.fori_loop(0, CH // 2, sent, 0)
+    lax.fori_loop(0, 2, sent_raw, 0)
     for i in range(4):
         relay(i).wait_send()
     for copy in results:
@@ -781,9 +841,10 @@
 ):
     loads, stores = [], []
     for i, (src, dst) in enumerate(((i_val, o_val), (i_gin, o_gin), (i_gout, o_gout))):
-        for n in range(2):
-            loads.append(pltpu.make_async_copy(src.at[n], stage.at[i, n], in_sem.at[2 * i + n]))
-            stores.append(pltpu.make_async_copy(stage.at[i, n], dst.at[n], out_sem.at[2 * i + n]))
+        for q in range(4):
+            part = (q // 2, pl.ds(q % 2 * (A // 2), A // 2))
+            loads.append(pltpu.make_async_copy(src.at[part], stage.at[(i,) + part], in_sem.at[4 * i + q]))
+            stores.append(pltpu.make_async_copy(stage.at[(i,) + part], dst.at[part], out_sem.at[4 * i + q]))
     small = [
         pltpu.make_async_copy(i_second, second, small_sem.at[0]),
         pltpu.make_async_copy(i_third, third, small_sem.at[1]),
@@ -852,7 +913,7 @@
         out_specs=[HB] * 3 + [VM] * 3,
         scratch_shapes=[pltpu.VMEM(shape, dtype) for shape, dtype in SCRATCH.values()]
         + [
-            DMA((N_LOCAL,)), DMA((6,)), DMA((5, 4)), DMA((5, 4)), DMA((4,)), DMA((4,)),
+            DMA((N_LOCAL,)), DMA((6,)), DMA((5, 4)), DMA((6, 4)), DMA((6, 2)), DMA((4,)), DMA((4,)),
             DMA((4, 4)), DMA((4, 4)), DMA((4, 5)), DMA((4, 5)), DMA((NSEQ,)), DMA((NSEQ,)),
             DMA((NSEQ,)), DMA((NSEQ,)), DMA((NCHAN,)), DMA((NCHAN,)), DMA((NSEQ,)), DMA((NSEQ,)),
         ],
@@ -874,7 +935,7 @@
             pltpu.VMEM((1, CH), F32), pltpu.VMEM((33, 64), F32), pltpu.VMEM((1, 64), F32),
             pltpu.VMEM((2, 64, 64), F32), pltpu.VMEM((2, 64), F32), pltpu.VMEM((64, 128), F32),
             pltpu.VMEM((1, 128), F32),
-            DMA((6,)), DMA((6,)), DMA((10,)),
+            DMA((12,)), DMA((12,)), DMA((10,)),
         ],
         compiler_params=pltpu.CompilerParams(vmem_limit_bytes=VMEM_MAIN),
         name="write_results",

time: 55.2 us -> 57.1 us (1.034)
  Pallas kernels: 54.4 us -> 56.3 us
    pallas_call x1, Pallas kernels: 51.5 us -> 53.4 us  [local(): pl.pallas_call(main_kernel, out_shape=[big, big, big, sds((8, 2, 8, 128))...]
where the time goes in v4:
time: 57.1 us; the launch traced here: 57 us
  Pallas kernels  56.3 us (99%)
  between operations  0.66 us (1%)
    pallas_call x1, Pallas kernels, local(): pl.pallas_call(main_kernel, out_shape=[big, big, big, sds((8, 2, 8, 128))...  53.4 us
    pallas_call x1, Pallas kernels, local(): pl.pallas_call(write_kernel, out_shape=[big, big, big, sds((1, CH)), sds(...  2.98 us

profile of v4, /device:TPU:1, one launch (start us, length us, event | category | flops | bytes accessed | tf_op | source)
XLA Modules:
  0.0 57.0 jit_solution(4753655135973305949)
XLA Ops:
  0.6 53.4 %hyena_backward.1 = (bf16[2,256,8,128]{3,2,1,0:T(8,128)(2,1)}, bf16[2,256,8,128]{3,2,1,0:T(8,128)(2,1)}, bf16[2,256,8,128]{3,2,1,0:T(8,128)(2,1)}, f32[8,2,8,128...) custom-call(s32[2,48,128]{2,1,0:T(8,128)} %constant.12.clone.refs_0_, f32[33,64]{1,0:T(8,128)} %bitcast.36, ...), custom_call_target="tpu_custom_call" | custom-call | tf_op jit(solution)/shard_map/hyena_backward/pallas_call | solution.py:909
  54.0 3.0 %write_results.1 = (bf16[2,256,8,128]{3,2,1,0:T(8,128)(2,1)}, bf16[2,256,8,128]{3,2,1,0:T(8,128)(2,1)}, bf16[2,256,8,128]{3,2,1,0:T(8,128)(2,1)}, f32[1,8]{1,0:T...) custom-call(bf16[2,256,8,128]{3,2,1,0:T(8,128)(2,1)} %get-tuple-elem, ...), custom_call_target="tpu_custom_call" | custom-call | tf_op jit(solution)/shard_map/write_results/pallas_call | solution.py:925

commit v5 on v4

--- a/solution.py
+++ b/solution.py
@@ -492,7 +492,7 @@
     names = list(SCRATCH)
     scratch = refs[N_LOCAL + len(OUTS) :]
     r = Refs(**dict(zip(OUTS, outs)), **dict(zip(names, scratch)))
-    (load_sem, out_sem, ag_send, ag_recv, cross_send, relay_send, relay_recv, half_send, half_recv, rs_send, rs_recv,
+    (load_sem, out_sem, ag_send, ag_recv, cross_send, cross_recv, relay_send, relay_recv, half_send, half_recv, rs_send, rs_recv,
      sem_a, recv_a, sem_b, recv_b, sem_c, recv_c, sem_d, recv_d) = scratch[len(names) :]
     r.raw_flat = r.raw_all.reshape(A * CH, B)
     chan, seq = lax.axis_index("chan"), lax.axis_index("seq")
@@ -509,7 +509,7 @@
     other = 1 - z
     near_seq = (2 * x + other, 2 * xr + z, 2 * xr + other, 2 * xl + z, 2 * xl + other)
     near = tuple((chan, to) for to in near_seq)
-    across = tuple((2 * yz + 1 - core, to) for to in near_seq + (seq,))
+    partner = (2 * yz + 1 - core, seq)
     to_r, to_l = near[1], near[3]
 
     def seq_peer(d):
@@ -539,8 +539,6 @@
         loads[name].start()
     lax.fori_loop(1, 8, hail, 0)
     lax.fori_loop(1, 16, hail_second, 0)
-    for i in range(5):
-        signal(across[i])
     for name in LARGE + TABLES:
         loads[name].start()
     for name in SMALL:
@@ -553,45 +551,43 @@
     def row_of(xx, zz):
         return (2 * xx + zz) * ABLK
 
-    def gather(i, j):
+    def gather(i, j, device=None):
         part = r.raw_all.at[pl.ds(row_of(x, z) + j * piece, piece)]
         return pltpu.make_async_remote_copy(
             src_ref=part, dst_ref=part, send_sem=ag_send.at[i, j], recv_sem=ag_recv.at[i, j],
-            device_id=near[i], device_id_type=MESH,
+            device_id=device or near[i], device_id_type=MESH,
         )
 
-    def cross(i, j):
+    def cross(j):
         return pltpu.make_async_remote_copy(
             src_ref=r.raw_other.at[pl.ds(j * piece, piece)],
             dst_ref=r.raw_all.at[pl.ds(row_of(x, z) + (2 * core + j) * piece, piece)],
-            send_sem=cross_send.at[i, j], recv_sem=ag_recv.at[i, 2 * core + j],
-            device_id=across[i], device_id_type=MESH,
+            send_sem=cross_send.at[j], recv_sem=cross_recv.at[j],
+            device_id=partner, device_id_type=MESH,
         )
 
     def send_chunk(j):
+        cross(j).start()
         for i in range(5):
             gather(i, 2 * core + j).start()
-        for i in range(6):
-            cross(i, j).start()
-
-    def relay(i):
-        row = row_of(xl if i < 2 else xr, (z, other)[i % 2]) + (0 if i < 2 else half)
+
+    def relay(h, lane):
+        row = jnp.where(h == 0, row_of(xl, (z, other)[lane]), row_of(xr, (z, other)[lane]) + half)
         part = r.raw_all.at[pl.ds(row, half)]
+        i = 2 * h + lane
         return pltpu.make_async_remote_copy(
             src_ref=part, dst_ref=part, send_sem=relay_send.at[i], recv_sem=relay_recv.at[i],
-            device_id=to_r if i < 2 else to_l, device_id_type=MESH,
+            device_id=(chan, jnp.where(h == 0, near_seq[1], near_seq[3])), device_id_type=MESH,
         )
 
-    def own_half(j):
-        part = r.raw_all.at[pl.ds(row_of(x, z) + (2 * (1 - core) + j) * piece, piece)]
-        return pltpu.make_async_remote_copy(
-            src_ref=part, dst_ref=part, send_sem=cross_send.at[5, j], recv_sem=ag_recv.at[5, 2 * (1 - core) + j],
-            device_id=across[5], device_id_type=MESH,
-        )
+    def pass_on(h):
+        for lane in range(2):
+            arrived(1 + 2 * h + lane, 2 * h, 2 * h + 2)
+            relay(h, lane).start()
 
     def arrived(i, start, stop):
         def step(j, carry):
-            gather(i, j).wait_recv()
+            gather(i, j, partner).wait_recv()
             return carry
 
         lax.fori_loop(start, stop, step, 0)
@@ -637,8 +633,13 @@
             near_block(p, i).start()
 
     prepare_weights(r, chan, 2 * yz + 1 - core)
-    pl.semaphore_wait(barrier, 7 + 7 + 15 + 5)
+    pl.semaphore_wait(barrier, 7 + 7 + 15)
     net_forward(r, seq, core, send_chunk)
+
+    for j in range(2):
+        cross(j).wait_recv()
+        for i in range(5):
+            gather(i, 2 * (1 - core) + j).start()
 
     for name in LARGE:
         loads[name].wait()
@@ -647,18 +648,13 @@
     r.skip_part[...] = jnp.sum(acc, axis=1, keepdims=True)
     for name in TABLES:
         loads[name].wait()
-    for i in range(2):
-        arrived(1 + i, 0, n_piece // 2)
-        relay(i).start()
 
     spectra(r, 0)
     scatter_far(0)
-    for i in range(2):
-        arrived(3 + i, n_piece // 2, n_piece)
-        relay(2 + i).start()
-
+    pass_on(core)
     spectra(r, 1)
     scatter_far(1)
+    pass_on(1 - core)
 
     def pair_step(p, carry):
         spectra(r, p)
@@ -667,14 +663,14 @@
         return carry
 
     lax.fori_loop(2, CH // 2, pair_step, 0)
+    scatter_near(CH // 2 - 2)
     arrived(0, 0, n_piece)
-    for j in range(2):
-        own_half(j).wait_recv()
-    for i in range(2):
-        arrived(1 + i, n_piece // 2, n_piece)
-        arrived(3 + i, 0, n_piece // 2)
-    for i in range(4):
-        relay(i).wait_recv()
+    for lane in range(2):
+        arrived(1 + lane, n_piece // 2, n_piece)
+        arrived(3 + lane, 0, n_piece // 2)
+    for h in range(2):
+        for lane in range(2):
+            relay(h, lane).wait_recv()
 
     def stats_step(c, carry):
         channel_stats(r, c)
@@ -702,18 +698,14 @@
 
     wait_along = run(NSEQ, make_a)
 
+    filter_products(r, 0)
+    scatter_near(CH // 2 - 1)
+
     def product_step(p, carry):
         filter_products(r, p)
-        scatter_near(p + CH // 2 - 2)
-        return carry
-
-    lax.fori_loop(0, 2, product_step, 0)
-
-    def last_step(p, carry):
-        filter_products(r, p)
-        return carry
-
-    lax.fori_loop(2, CH // 2, last_step, 0)
+        return carry
+
+    lax.fori_loop(1, CH // 2, product_step, 0)
     results = []
 
     def leave(n):
@@ -759,7 +751,7 @@
     gradient(1 - core)
     hand = pltpu.make_async_remote_copy(
         src_ref=r.grad_own.at[pl.ds((1 - core) * half, half)], dst_ref=r.grad_other,
-        send_sem=sem_a.at[0], recv_sem=recv_a.at[0], device_id=across[5], device_id_type=MESH,
+        send_sem=sem_a.at[0], recv_sem=recv_a.at[0], device_id=partner, device_id_type=MESH,
     )
     hand.start()
     gradient(core)
@@ -768,15 +760,9 @@
     def sent(j, carry):
         for i in range(5):
             near_block(j, i).wait_send()
+            gather(i, j).wait_send()
         for i in range(4):
             far_half(j, i // 2, i % 2).wait_send()
-        return carry
-
-    def sent_raw(j, carry):
-        for i in range(5):
-            gather(i, 2 * core + j).wait_send()
-        for i in range(6):
-            cross(i, j).wait_send()
         return carry
 
     net_backward(r, seq, core)
@@ -827,9 +813,10 @@
     wait()
     swap.wait()
     lax.fori_loop(0, CH // 2, sent, 0)
-    lax.fori_loop(0, 2, sent_raw, 0)
-    for i in range(4):
-        relay(i).wait_send()
+    for i in range(2):
+        cross(i).wait_send()
+        for lane in range(2):
+            relay(i, lane).wait_send()
     for copy in results:
         copy.wait()
 
@@ -913,7 +900,7 @@
         out_specs=[HB] * 3 + [VM] * 3,
         scratch_shapes=[pltpu.VMEM(shape, dtype) for shape, dtype in SCRATCH.values()]
         + [
-            DMA((N_LOCAL,)), DMA((6,)), DMA((5, 4)), DMA((6, 4)), DMA((6, 2)), DMA((4,)), DMA((4,)),
+            DMA((N_LOCAL,)), DMA((6,)), DMA((5, 4)), DMA((5, 4)), DMA((2,)), DMA((2,)), DMA((4,)), DMA((4,)),
             DMA((4, 4)), DMA((4, 4)), DMA((4, 5)), DMA((4, 5)), DMA((NSEQ,)), DMA((NSEQ,)),
             DMA((NSEQ,)), DMA((NSEQ,)), DMA((NCHAN,)), DMA((NCHAN,)), DMA((NSEQ,)), DMA((NSEQ,)),
         ],

time: 57.1 us -> 54.3 us (0.951)
  Pallas kernels: 56.3 us -> 53.5 us
    pallas_call x1, Pallas kernels: 53.4 us -> 50.5 us  [local(): pl.pallas_call(main_kernel, out_shape=[big, big, big, sds((8, 2, 8, 128))...]
where the time goes in v5:
time: 54.3 us; the launch traced here: 54.1 us
  Pallas kernels  53.5 us (99%)
  between operations  0.66 us (1%)
    pallas_call x1, Pallas kernels, local(): pl.pallas_call(main_kernel, out_shape=[big, big, big, sds((8, 2, 8, 128))...  50.5 us
    pallas_call x1, Pallas kernels, local(): pl.pallas_call(write_kernel, out_shape=[big, big, big, sds((1, CH)), sds(...  2.98 us

profile of v5, /device:TPU:1, one launch (start us, length us, event | category | flops | bytes accessed | tf_op | source)
XLA Modules:
  0.0 54.1 jit_solution(3264931113834501459)
XLA Ops:
  0.6 50.5 %hyena_backward.1 = (bf16[2,256,8,128]{3,2,1,0:T(8,128)(2,1)}, bf16[2,256,8,128]{3,2,1,0:T(8,128)(2,1)}, bf16[2,256,8,128]{3,2,1,0:T(8,128)(2,1)}, f32[8,2,8,128...) custom-call(s32[2,48,128]{2,1,0:T(8,128)} %constant.12.clone.refs_0_, f32[33,64]{1,0:T(8,128)} %bitcast.36, ...), custom_call_target="tpu_custom_call" | custom-call | tf_op jit(solution)/shard_map/hyena_backward/pallas_call | solution.py:896
  51.1 3.0 %write_results.1 = (bf16[2,256,8,128]{3,2,1,0:T(8,128)(2,1)}, bf16[2,256,8,128]{3,2,1,0:T(8,128)(2,1)}, bf16[2,256,8,128]{3,2,1,0:T(8,128)(2,1)}, f32[1,8]{1,0:T...) custom-call(bf16[2,256,8,128]{3,2,1,0:T(8,128)(2,1)} %get-tuple-elem, ...), custom_call_target="tpu_custom_call" | custom-call | tf_op jit(solution)/shard_map/write_results/pallas_call | solution.py:912

commit v6 on v5

--- a/solution.py
+++ b/solution.py
@@ -162,19 +162,25 @@
     for i in range(2):
         w = r.w_mid[i]
         r.k_mid[i] = hi_hi_lo(dot_full(w, rep), 64)
-        r.k_back[i] = hi_hi_lo(dot_tn(w, rep, HIGHEST), 64)
     row = iota((2 * CH, 128), 0)
     channel = jnp.where(row < CH, row + chan * CH, row - CH + other * CH)
     pick = jnp.where(iota((2 * CH, 128), 1) == channel, 1.0, 0.0)
     w_own = dot_nt(pick, r.w_out[...], HIGHEST)
     r.k_out[...] = hi_hi_lo(dot_full(w_own, rep), 64)
-    r.k_outback[...] = hi_hi_lo(dot_tn(w_own, repeat_matrix(2 * CH, 2 * CH, 3), HIGHEST), 2 * CH)
+    r.w_own[...] = w_own
     rates = jnp.sum(jnp.where(pick > 0.5, jnp.broadcast_to(r.rate[...], (2 * CH, 128)), 0.0), axis=1, keepdims=True)
     r.rate_col[...] = jnp.broadcast_to(rates, (2 * CH, 128))
     r.bias_col[0] = jnp.broadcast_to(to_column(r.b_mid[0:1, :], 64, 0), (64, 128))
     r.bias_col[1] = jnp.broadcast_to(to_column(r.b_mid[1:2, :], 64, 0), (64, 128))
 
 
+def prepare_backward(r):
+    rep = repeat_matrix(64, 64, 3)
+    for i in range(2):
+        r.k_back[i] = hi_hi_lo(dot_tn(r.w_mid[i], rep, HIGHEST), 64)
+    r.k_outback[...] = hi_hi_lo(dot_tn(r.w_own[...], repeat_matrix(2 * CH, 2 * CH, 3), HIGHEST), 2 * CH)
+
+
 def wide(block, times):
     return jnp.concatenate([block] * times, axis=1)
 
@@ -184,42 +190,35 @@
     return pos.astype(F32) * (1.0 / L)
 
 
-def net_forward(r, seq, core, send):
+def net_chunk(r, seq, core, j):
     per = CHUNK // 128
-
-    def step(j, carry):
-        base = pl.multiple_of(j * CHUNK, CHUNK)
-        lanes = pl.ds(base, CHUNK)
-        pos = seq * TB + (2 * core + j) * CHUNK + iota((48, CHUNK), 1)
-        row = iota((48, CHUNK), 0)
-        phase = ((wide(r.bands[0], per) * pos + (wide(r.bands[1], per) + L // 2)) & (L - 1)) - L // 2
-        phase = jnp.where(phase > L // 4, L // 2 - phase, phase)
-        phase = jnp.where(phase < -(L // 4), -(L // 2) - phase, phase)
-        wave = sin_small(phase.astype(F32) * (2.0 * math.pi / L))
-        frac = pos.astype(F32) * (1.0 / L)
-        hi, lo = split(jnp.where(row == 0, frac, jnp.where(row == 33, 1.0, wave)))
-        r.feat[0:48, lanes] = hi
-        r.feat[48:64, lanes] = jnp.zeros((16, CHUNK), LOW)
-        r.feat[64:112, lanes] = lo
-        r.feat[112:128, lanes] = jnp.zeros((16, CHUNK), LOW)
-        z = low_dot(r.k_in[...], jnp.concatenate([hi, lo, hi], axis=0))
-        for layer in range(3):
-            s, c = sin_cos(z)
-            r.der[layer, :, lanes] = c
-            hi, lo = split(s)
-            r.act[layer, 0:64, lanes] = hi
-            r.act[layer, 64:128, lanes] = lo
-            x = jnp.concatenate([hi, lo, hi], axis=0)
-            if layer < 2:
-                z = low_dot(r.k_mid[layer], x) + wide(r.bias_col[layer], per)
-        raw = low_dot(r.k_out[...], x) * jnp.exp(-wide(r.rate_col[...], per) * frac[0 : 2 * CH, :])
-        for i in range(per):
-            r.raw_all[seq * ABLK + (2 * core + j) * per + i] = raw[0:CH, 128 * i : 128 * i + 128]
-            r.raw_other[j * per + i] = raw[CH:, 128 * i : 128 * i + 128]
-        send(j)
-        return carry
-
-    lax.fori_loop(0, TB // CHUNK // 2, step, 0)
+    lanes = pl.ds(j * CHUNK, CHUNK)
+    pos = seq * TB + (2 * core + j) * CHUNK + iota((48, CHUNK), 1)
+    row = iota((48, CHUNK), 0)
+    phase = ((wide(r.bands[0], per) * pos + (wide(r.bands[1], per) + L // 2)) & (L - 1)) - L // 2
+    phase = jnp.where(phase > L // 4, L // 2 - phase, phase)
+    phase = jnp.where(phase < -(L // 4), -(L // 2) - phase, phase)
+    wave = sin_small(phase.astype(F32) * (2.0 * math.pi / L))
+    frac = pos.astype(F32) * (1.0 / L)
+    hi, lo = split(jnp.where(row == 0, frac, jnp.where(row == 33, 1.0, wave)))
+    r.feat[0:48, lanes] = hi
+    r.feat[48:64, lanes] = jnp.zeros((16, CHUNK), LOW)
+    r.feat[64:112, lanes] = lo
+    r.feat[112:128, lanes] = jnp.zeros((16, CHUNK), LOW)
+    z = low_dot(r.k_in[...], jnp.concatenate([hi, lo, hi], axis=0))
+    for layer in range(3):
+        s, c = sin_cos(z)
+        r.der[layer, :, lanes] = c
+        hi, lo = split(s)
+        r.act[layer, 0:64, lanes] = hi
+        r.act[layer, 64:128, lanes] = lo
+        x = jnp.concatenate([hi, lo, hi], axis=0)
+        if layer < 2:
+            z = low_dot(r.k_mid[layer], x) + wide(r.bias_col[layer], per)
+    raw = low_dot(r.k_out[...], x) * jnp.exp(-wide(r.rate_col[...], per) * frac[0 : 2 * CH, :])
+    for i in range(per):
+        r.raw_all[seq * ABLK + (2 * core + j) * per + i] = raw[0:CH, 128 * i : 128 * i + 128]
+        r.raw_other[j * per + i] = raw[CH:, 128 * i : 128 * i + 128]
 
 
 def net_backward(r, seq, core):
@@ -331,6 +330,8 @@
 
 
 BLK = 16
+EARLY = 2
+UNDER_FIRST = 1
 VMEM_MAIN = 56 << 20
 
 
@@ -449,6 +450,7 @@
     "k_in": ((64, 144), LOW),
     "k_mid": ((2, 64, 192), LOW),
     "k_back": ((2, 64, 192), LOW),
+    "w_own": ((2 * CH, 64), F32),
     "k_out": ((2 * CH, 192), LOW),
     "k_outback": ((64, 6 * CH), LOW),
     "rate_col": ((2 * CH, 128), F32),
@@ -633,14 +635,18 @@
             near_block(p, i).start()
 
     prepare_weights(r, chan, 2 * yz + 1 - core)
+    net_chunk(r, seq, core, 0)
     pl.semaphore_wait(barrier, 7 + 7 + 15)
-    net_forward(r, seq, core, send_chunk)
+    send_chunk(0)
+    net_chunk(r, seq, core, 1)
+    send_chunk(1)
 
     for j in range(2):
         cross(j).wait_recv()
         for i in range(5):
             gather(i, 2 * (1 - core) + j).start()
 
+    prepare_backward(r)
     for name in LARGE:
         loads[name].wait()
     acc = gate_products(r, 0)
@@ -705,7 +711,7 @@
         filter_products(r, p)
         return carry
 
-    lax.fori_loop(1, CH // 2, product_step, 0)
+    lax.fori_loop(1, EARLY, product_step, 0)
     results = []
 
     def leave(n):
@@ -713,9 +719,6 @@
             copy = pltpu.make_async_copy(src.at[n], dst.at[n], out_sem.at[3 * n + i])
             copy.start()
             results.append(copy)
-
-    finish(r, 0)
-    leave(0)
 
     def settle(p, carry):
         for i in range(5):
@@ -746,7 +749,7 @@
             r.grad_own[row] = total * scale_gk - r.raw_all[row_of(x, z) + row] * scale_raw
             return carry
 
-        lax.fori_loop(0, half, step, 0, unroll=4)
+        lax.fori_loop(0, half, step, 0, unroll=8)
 
     gradient(1 - core)
     hand = pltpu.make_async_remote_copy(
@@ -787,15 +790,19 @@
         )
 
     wait = run(8, make_b)
-    finish(r, 1)
-    leave(1)
+    lax.fori_loop(EARLY, EARLY + UNDER_FIRST, product_step, 0)
     wait()
     both = r.share[first_id]
     for d in range(1, 8):
         both = both + r.first[d]
     factor = 1.0 / math.sqrt(16 * L)
     r.second[second_id] = both * factor
-    run(16, make_c)()
+    wait = run(16, make_c)
+    lax.fori_loop(EARLY + UNDER_FIRST, CH // 2, product_step, 0)
+    for n in range(2):
+        finish(r, n)
+        leave(n)
+    wait()
     total = r.second[0]
     for c in range(1, 16):
         total = total + r.second[c]

time: 54.3 us -> 52.8 us (0.972)
  Pallas kernels: 53.5 us -> 51.8 us
    pallas_call x1, Pallas kernels: 50.5 us -> 48.8 us  [local(): pl.pallas_call(main_kernel, out_shape=[big, big, big, sds((8, 2, 8, 128))...]
where the time goes in v6:
time: 52.8 us; the launch traced here: 52.6 us
  Pallas kernels  51.8 us (98%)
  between operations  0.82 us (2%)
    pallas_call x1, Pallas kernels, local(): pl.pallas_call(main_kernel, out_shape=[big, big, big, sds((8, 2, 8, 128))...  48.8 us
    pallas_call x1, Pallas kernels, local(): pl.pallas_call(write_kernel, out_shape=[big, big, big, sds((1, CH)), sds(...  2.98 us

profile of v6, /device:TPU:1, one launch (start us, length us, event | category | flops | bytes accessed | tf_op | source)
XLA Modules:
  0.0 52.6 jit_solution(9585801717749346573)
XLA Ops:
  0.6 48.8 %hyena_backward.1 = (bf16[2,256,8,128]{3,2,1,0:T(8,128)(2,1)}, bf16[2,256,8,128]{3,2,1,0:T(8,128)(2,1)}, bf16[2,256,8,128]{3,2,1,0:T(8,128)(2,1)}, f32[8,2,8,128...) custom-call(s32[2,48,128]{2,1,0:T(8,128)} %constant.12.clone.refs_0_, f32[33,64]{1,0:T(8,128)} %bitcast.36, ...), custom_call_target="tpu_custom_call" | custom-call | tf_op jit(solution)/shard_map/hyena_backward/pallas_call | solution.py:903
  49.5 3.0 %write_results.1 = (bf16[2,256,8,128]{3,2,1,0:T(8,128)(2,1)}, bf16[2,256,8,128]{3,2,1,0:T(8,128)(2,1)}, bf16[2,256,8,128]{3,2,1,0:T(8,128)(2,1)}, f32[1,8]{1,0:T...) custom-call(bf16[2,256,8,128]{3,2,1,0:T(8,128)(2,1)} %get-tuple-elem, ...), custom_call_target="tpu_custom_call" | custom-call | tf_op jit(solution)/shard_map/write_results/pallas_call | solution.py:919

commit v7 on v6

--- a/solution.py
+++ b/solution.py
@@ -265,7 +265,7 @@
                 r.acc[0] += dot_nt(pair, r.feat[:, lanes])
         return carry
 
-    lax.fori_loop(0, TB // CHUNK // 2, step, 0)
+    lax.fori_loop(0, TB // CHUNK // 2, step, 0, unroll=True)
 
 
 def fold_halves(x):
@@ -570,7 +570,7 @@
 
     def send_chunk(j):
         cross(j).start()
-        for i in range(5):
+        for i in (1, 3, 2, 4, 0):
             gather(i, 2 * core + j).start()
 
     def relay(h, lane):
@@ -643,7 +643,7 @@
 
     for j in range(2):
         cross(j).wait_recv()
-        for i in range(5):
+        for i in (1, 3, 2, 4, 0):
             gather(i, 2 * (1 - core) + j).start()
 
     prepare_backward(r)
@@ -656,11 +656,11 @@
         loads[name].wait()
 
     spectra(r, 0)
+    pass_on(core)
     scatter_far(0)
-    pass_on(core)
     spectra(r, 1)
+    pass_on(1 - core)
     scatter_far(1)
-    pass_on(1 - core)
 
     def pair_step(p, carry):
         spectra(r, p)
@@ -682,7 +682,7 @@
         channel_stats(r, c)
         return carry
 
-    lax.fori_loop(0, CH, stats_step, 0)
+    lax.fori_loop(0, CH, stats_step, 0, unroll=2)
 
     def run(size, make):
         def start(d, carry):
@@ -732,7 +732,7 @@
             r.total[pl.ds(pl.multiple_of(c * ABLK, ABLK), ABLK), :] = total
         return carry
 
-    lax.fori_loop(0, CH // 2, settle, 0)
+    lax.fori_loop(0, CH // 2, settle, 0, unroll=True)
     wait_along()
     along = r.stat[1]
     for d in range(1, NSEQ):
@@ -749,7 +749,7 @@
             r.grad_own[row] = total * scale_gk - r.raw_all[row_of(x, z) + row] * scale_raw
             return carry
 
-        lax.fori_loop(0, half, step, 0, unroll=8)
+        lax.fori_loop(0, half, step, 0, unroll=True)
 
     gradient(1 - core)
     hand = pltpu.make_async_remote_copy(

time: 52.8 us -> 52.2 us (0.989)
    pallas_call x1, Pallas kernels: 48.8 us -> 48.3 us  [local(): pl.pallas_call(main_kernel, out_shape=[big, big, big, sds((8, 2, 8, 128))...]
where the time goes in v7:
time: 52.2 us; the launch traced here: 52.1 us
  Pallas kernels  51.3 us (98%)
  between operations  0.82 us (2%)
    pallas_call x1, Pallas kernels, local(): pl.pallas_call(main_kernel, out_shape=[big, big, big, sds((8, 2, 8, 128))...  48.3 us
    pallas_call x1, Pallas kernels, local(): pl.pallas_call(write_kernel, out_shape=[big, big, big, sds((1, CH)), sds(...  2.98 us

profile of v7, /device:TPU:1, one launch (start us, length us, event | category | flops | bytes accessed | tf_op | source)
XLA Modules:
  0.0 52.1 jit_solution(2428563318623063760)
XLA Ops:
  0.6 48.3 %hyena_backward.1 = (bf16[2,256,8,128]{3,2,1,0:T(8,128)(2,1)}, bf16[2,256,8,128]{3,2,1,0:T(8,128)(2,1)}, bf16[2,256,8,128]{3,2,1,0:T(8,128)(2,1)}, f32[8,2,8,128...) custom-call(s32[2,48,128]{2,1,0:T(8,128)} %constant.12.clone.refs_0_, f32[33,64]{1,0:T(8,128)} %bitcast.36, ...), custom_call_target="tpu_custom_call" | custom-call | tf_op jit(solution)/shard_map/hyena_backward/pallas_call | solution.py:903
  48.9 3.0 %write_results.1 = (bf16[2,256,8,128]{3,2,1,0:T(8,128)(2,1)}, bf16[2,256,8,128]{3,2,1,0:T(8,128)(2,1)}, bf16[2,256,8,128]{3,2,1,0:T(8,128)(2,1)}, f32[1,8]{1,0:T...) custom-call(bf16[2,256,8,128]{3,2,1,0:T(8,128)(2,1)} %get-tuple-elem, ...), custom_call_target="tpu_custom_call" | custom-call | tf_op jit(solution)/shard_map/write_results/pallas_call | solution.py:919

commit v8 on v7

--- a/solution.py
+++ b/solution.py
@@ -817,8 +817,6 @@
     )
     swap.start()
     r.g_skip[...] = to_row(r.own[yz, core][:, 113:114])
-    wait()
-    swap.wait()
     lax.fori_loop(0, CH // 2, sent, 0)
     for i in range(2):
         cross(i).wait_send()
@@ -826,6 +824,8 @@
             relay(i, lane).wait_send()
     for copy in results:
         copy.wait()
+    wait()
+    swap.wait()
 
 
 def write_kernel(

time: 52.2 us -> 52.1 us (level)
  no operation moved by 1% of the time
where the time goes in v8:
time: 52.1 us; the launch traced here: 52 us
  Pallas kernels  51.1 us (98%)
  between operations  0.82 us (2%)
    pallas_call x1, Pallas kernels, local(): pl.pallas_call(main_kernel, out_shape=[big, big, big, sds((8, 2, 8, 128))...  48.2 us
    pallas_call x1, Pallas kernels, local(): pl.pallas_call(write_kernel, out_shape=[big, big, big, sds((1, CH)), sds(...  2.98 us

profile of v8, /device:TPU:1, one launch (start us, length us, event | category | flops | bytes accessed | tf_op | source)
XLA Modules:
  0.0 52.0 jit_solution(12134155119585505581)
XLA Ops:
  0.6 48.2 %hyena_backward.1 = (bf16[2,256,8,128]{3,2,1,0:T(8,128)(2,1)}, bf16[2,256,8,128]{3,2,1,0:T(8,128)(2,1)}, bf16[2,256,8,128]{3,2,1,0:T(8,128)(2,1)}, f32[8,2,8,128...) custom-call(s32[2,48,128]{2,1,0:T(8,128)} %constant.12.clone.refs_0_, f32[33,64]{1,0:T(8,128)} %bitcast.36, ...), custom_call_target="tpu_custom_call" | custom-call | tf_op jit(solution)/shard_map/hyena_backward/pallas_call | solution.py:903
  48.8 3.0 %write_results.1 = (bf16[2,256,8,128]{3,2,1,0:T(8,128)(2,1)}, bf16[2,256,8,128]{3,2,1,0:T(8,128)(2,1)}, bf16[2,256,8,128]{3,2,1,0:T(8,128)(2,1)}, f32[1,8]{1,0:T...) custom-call(bf16[2,256,8,128]{3,2,1,0:T(8,128)(2,1)} %get-tuple-elem, ...), custom_call_target="tpu_custom_call" | custom-call | tf_op jit(solution)/shard_map/write_results/pallas_call | solution.py:919
